TPU v7x, 128 devices: a whole 4x4x4 slice. The times are simulated.
128 devices in a mesh: comp: 2 (over core), tile: 64 (over x, z, y).
Axes of the slice: x: 4, y: 4, z: 4, core: 2. Of those that a mesh axis runs over, the one named last changes fastest.
Arguments:
- state: float32 [2, 1024, 256], P('comp', 'tile'), may hold values from -6 to 6
- coeff: float32 [2, 1024, 256], P('comp', 'tile'), may hold values from 0.3 to 3
- vertical: int32 [1024, 256], P('tile'), may hold values from 0 to 5
- send_cell: int32 [1024, 4096], P(('comp', 'tile')), may hold values from 0 to 4095, as said below
- incoming_marine_slot: int32 [1024, 4096], P(('comp', 'tile')), may hold values from 0 to 4095, as said below
- remap_weight: float32 [1024, 4096], P(('comp', 'tile')), as said below
Outputs:
- exchanged_pair: float32 [2, 1024, 256], P('comp', 'tile')
Inputs may be any that keep to these rules, and one draw needn't show every extreme that they name: `send_cell`: rows of ocean partitions (index 512 and above) are 0. Rows d = 3 and d = 5 of every atmosphere partition are full; rows 0 and 1, 2 and 4, 6 and 7 come in pairs whose live slots fill one row together. Live slots lead each row; dead slots hold cell 0. Every atmosphere cell is named by exactly five live slots of its partition. `incoming_marine_slot`: rows of atmosphere partitions are 0. Row (64 + t) * 8 + d names the ocean cell of the slot that send_cell row ((t - d + 4) mod 64) * 8 + d names; dead slots hold 0. `remap_weight`: live slots have weights of at least 0.25; dead slots and rows of ocean partitions 0.
All inputs are finite; a program needn't handle non-finite values.
Results may differ from a plain program's by a relative error of at most 0.00002.
Values sent between devices are 32-bit elements; how exact they have to be, the bound alone decides.
A program may use at most 64 MiB of HBM per device.

v0:
```python
import jax
import jax.numpy as jnp
from jax import lax
from jax.sharding import PartitionSpec as P

SPAN = 8
SWEEPS = 20


def with_halo(array, sides, width):
    for axis, dim in sides:
        devices, length = (lax.axis_size(axis), array.shape[dim])
        up = [(i, (i + 1) % devices) for i in range(devices)]
        down = [(j, i) for i, j in up]
        last = lax.slice_in_dim(array, length - width, length, axis=dim)
        initial = lax.slice_in_dim(array, 0, width, axis=dim)
        before = lax.ppermute(last, axis, up)
        after = lax.ppermute(initial, axis, down)
        array = jnp.concatenate([before, array, after], axis=dim)
    return array


def shards(state, coeff, vertical, send_cell, incoming_marine_slot, remap_weight):
    mesh_lines = state.shape[1]
    line_length = state.shape[2]
    cells = mesh_lines * line_length
    tiles = lax.axis_size("tile")
    model_index = lax.axis_index("comp")
    tile_index = lax.axis_index("tile")
    middle = SPAN // 2
    mesh_quantity = state[0]
    rate = coeff[0]
    padded = with_halo(mesh_quantity, (("tile", 0),), 1)
    near = padded[:-2] + padded[2:] + jnp.roll(mesh_quantity, 1, 1) + jnp.roll(mesh_quantity, -1, 1)
    air_flux = (rate * (mesh_quantity + 0.2 * (near - 4.0 * mesh_quantity))).reshape(-1)
    offsets = jnp.arange(SPAN, dtype=jnp.int32)
    ahead_rows = tiles + (tile_index + offsets - middle) % tiles
    behind_rows = (tile_index - offsets + middle) % tiles
    zeros_flat = jnp.zeros((cells,), jnp.float32)
    outgoing = remap_weight * jnp.take(air_flux, send_cell)
    buffer = jnp.zeros((2 * tiles, cells), jnp.float32).at[ahead_rows].set(outgoing)
    arrived = lax.all_to_all(buffer, ("comp", "tile"), split_axis=0, concat_axis=0, tiled=True)
    incoming = arrived[behind_rows]
    ocean_source = zeros_flat.at[incoming_marine_slot.reshape(-1)].add(incoming.reshape(-1))
    source_mesh = ocean_source.reshape(mesh_lines, line_length)
    rhs = source_mesh + mesh_quantity
    diag = rate + 3.0
    col_ids = jnp.arange(line_length, dtype=jnp.int32)[None, :]
    zeros_grid = jnp.zeros((mesh_lines, line_length), jnp.float32)
    row_ids = jnp.arange(mesh_lines, dtype=jnp.int32)[:, None]
    up_down = vertical // 3
    sideways = vertical % 3 - 1
    index = (row_ids + 2 * up_down) * line_length + (col_ids + sideways) % line_length

    def sweep_once(step, skin_quantity):
        extended = with_halo(skin_quantity, (("tile", 0),), 1)
        beside_all = (
            jnp.roll(skin_quantity, 1, 1)
            + jnp.roll(skin_quantity, -1, 1)
            + jnp.take(extended.reshape(-1), index)
        )
        return (rhs + beside_all) / diag

    skin_quantity = lax.fori_loop(0, SWEEPS, sweep_once, zeros_grid)
    linear_skin_heat = (mesh_quantity + 0.5 * skin_quantity - 0.25 * source_mesh).reshape(-1)
    share_accumulated = zeros_flat.at[send_cell.reshape(-1)].add(remap_weight.reshape(-1))
    backward_transfers = jnp.take(linear_skin_heat, incoming_marine_slot)
    buffer_back = jnp.zeros((2 * tiles, cells), jnp.float32).at[behind_rows].set(backward_transfers)
    arrived_back = lax.all_to_all(
        buffer_back, ("comp", "tile"), split_axis=0, concat_axis=0, tiled=True
    )
    incoming_back = arrived_back[ahead_rows]
    overall_quantity = zeros_flat.at[send_cell.reshape(-1)].add(
        (remap_weight * incoming_back).reshape(-1)
    )
    safe_share_total = share_accumulated + (model_index != 0).astype(jnp.float32)
    measured_skin_heat = (overall_quantity / safe_share_total).reshape(mesh_lines, line_length)
    exchanged_pair = jnp.where(model_index == 0, measured_skin_heat, skin_quantity)
    return exchanged_pair[None]


def solution(mesh):
    in_specs = (
        P("comp", "tile", None),
        P("comp", "tile", None),
        P("tile", None),
        P(("comp", "tile"), None),
        P(("comp", "tile"), None),
        P(("comp", "tile"), None),
    )
    out_specs = P("comp", "tile", None)
    return jax.shard_map(shards, mesh=mesh, in_specs=in_specs, out_specs=out_specs, check_vma=False)
```

profile of v0, /device:TPU:0, one launch (start us, length us, event | category | flops | bytes accessed | tf_op | source)
XLA Modules:
  0.0 1741.1 jit_solution(4828873816752332242)
XLA Ops:
  14.2 180.5 %gather_fusion.3 = f32[32768]{0:T(1024)S(1)} fusion(f32[4096]{0:T(1024)S(1)} %bitcast.64, s32[32768]{0:T(1024)S(1)} %broadcast_clamp_fusion.2), kind=kCustom, calls=%fused_computation.clone | custom fusion | bytes 393216 | tf_op jit(solution)/shard_map/jit(_take)/gather | solution.py:40
  207.4 29.7 %all-to-all-done = f32[128,1,4096]{2,1,0:T(1,128)S(1)} async-done(((f32[128,1,4096]{2,1,0:T(1,128)}), f32[128,1,4096]{2,1,0:T(1,128)S(1)}, u32[]{:S(2)}, u32[]{:S(2)}) %all-to-all-start) | async-done | bytes 2097184 | tf_op jit(solution)/shard_map/all_to_all | solution.py:42
  242.4 226.3 %scatter_custom_fusion.1 = f32[4096]{0:T(1024)S(1)} fusion(s32[32768]{0:T(1024)S(1)} %bitcast.83, f32[32768]{0:T(1024)S(1)} %bitcast.85, f32[]{:T(128)} %constant.102.clone.1), kind=kCustom, calls=%fused_computation.83 | custom fusion | flops 32768 | bytes 16388 | tf_op jit(solution)/shard_map/scatter-add | solution.py:44
  468.8 649.7 %while.11 = (s32[]{:T(128)}, f32[16,256]{1,0:T(8,128)S(1)}, s32[16,256]{1,0:T(8,128)S(1)}, f32[16,256]{1,0:T(8,128)S(1)}, f32[16,256]{1,0:T(8,128)S(1)}, /*index=5*/s32[]{:T(128)}, s32[]{:T(128)}) while((s32[]{:T(128)}, f32[16,256]{1,0:T(8,128)S(1)}, s32[16,256]{1,0:T(8,128)S(1)}, f32[16,256]{1,0:T(8,128)S(1)}, ...), condition=%wide.region_3.5_spmd.clone, body=%wide.region_2.4_spmd.clone.sunk | while | flops 82947 | bytes 479399 | solution.py:64
  481.1 23.0 %gather_fusion = f32[4096]{0:T(1024)S(1)} fusion(f32[4608]{0:T(1024)S(1)} %reshape.349, s32[4096]{0:T(1024)S(1)} %broadcast_clamp_fusion.4), kind=kCustom, calls=%fused_computation.1.clone.clone.1 | custom fusion | bytes 49152 | tf_op jit(solution)/shard_map/while/body/eval_jaxpr/jit(_take)/gather | solution.py:60
  513.5 23.0 %gather_fusion = f32[4096]{0:T(1024)S(1)} fusion(f32[4608]{0:T(1024)S(1)} %reshape.349, s32[4096]{0:T(1024)S(1)} %broadcast_clamp_fusion.4), kind=kCustom, calls=%fused_computation.1.clone.clone.1 | custom fusion | bytes 49152 | tf_op jit(solution)/shard_map/while/body/eval_jaxpr/jit(_take)/gather | solution.py:60
  545.8 23.0 %gather_fusion = f32[4096]{0:T(1024)S(1)} fusion(f32[4608]{0:T(1024)S(1)} %reshape.349, s32[4096]{0:T(1024)S(1)} %broadcast_clamp_fusion.4), kind=kCustom, calls=%fused_computation.1.clone.clone.1 | custom fusion | bytes 49152 | tf_op jit(solution)/shard_map/while/body/eval_jaxpr/jit(_take)/gather | solution.py:60
  578.1 23.0 %gather_fusion = f32[4096]{0:T(1024)S(1)} fusion(f32[4608]{0:T(1024)S(1)} %reshape.349, s32[4096]{0:T(1024)S(1)} %broadcast_clamp_fusion.4), kind=kCustom, calls=%fused_computation.1.clone.clone.1 | custom fusion | bytes 49152 | tf_op jit(solution)/shard_map/while/body/eval_jaxpr/jit(_take)/gather | solution.py:60
  642.7 23.0 %gather_fusion = f32[4096]{0:T(1024)S(1)} fusion(f32[4608]{0:T(1024)S(1)} %reshape.349, s32[4096]{0:T(1024)S(1)} %broadcast_clamp_fusion.4), kind=kCustom, calls=%fused_computation.1.clone.clone.1 | custom fusion | bytes 49152 | tf_op jit(solution)/shard_map/while/body/eval_jaxpr/jit(_take)/gather | solution.py:60
  707.4 23.0 %gather_fusion = f32[4096]{0:T(1024)S(1)} fusion(f32[4608]{0:T(1024)S(1)} %reshape.349, s32[4096]{0:T(1024)S(1)} %broadcast_clamp_fusion.4), kind=kCustom, calls=%fused_computation.1.clone.clone.1 | custom fusion | bytes 49152 | tf_op jit(solution)/shard_map/while/body/eval_jaxpr/jit(_take)/gather | solution.py:60
  739.7 23.0 %gather_fusion = f32[4096]{0:T(1024)S(1)} fusion(f32[4608]{0:T(1024)S(1)} %reshape.349, s32[4096]{0:T(1024)S(1)} %broadcast_clamp_fusion.4), kind=kCustom, calls=%fused_computation.1.clone.clone.1 | custom fusion | bytes 49152 | tf_op jit(solution)/shard_map/while/body/eval_jaxpr/jit(_take)/gather | solution.py:60
  772.0 23.0 %gather_fusion = f32[4096]{0:T(1024)S(1)} fusion(f32[4608]{0:T(1024)S(1)} %reshape.349, s32[4096]{0:T(1024)S(1)} %broadcast_clamp_fusion.4), kind=kCustom, calls=%fused_computation.1.clone.clone.1 | custom fusion | bytes 49152 | tf_op jit(solution)/shard_map/while/body/eval_jaxpr/jit(_take)/gather | solution.py:60
  804.4 23.0 %gather_fusion = f32[4096]{0:T(1024)S(1)} fusion(f32[4608]{0:T(1024)S(1)} %reshape.349, s32[4096]{0:T(1024)S(1)} %broadcast_clamp_fusion.4), kind=kCustom, calls=%fused_computation.1.clone.clone.1 | custom fusion | bytes 49152 | tf_op jit(solution)/shard_map/while/body/eval_jaxpr/jit(_take)/gather | solution.py:60
  836.7 23.0 %gather_fusion = f32[4096]{0:T(1024)S(1)} fusion(f32[4608]{0:T(1024)S(1)} %reshape.349, s32[4096]{0:T(1024)S(1)} %broadcast_clamp_fusion.4), kind=kCustom, calls=%fused_computation.1.clone.clone.1 | custom fusion | bytes 49152 | tf_op jit(solution)/shard_map/while/body/eval_jaxpr/jit(_take)/gather | solution.py:60
  869.0 23.0 %gather_fusion = f32[4096]{0:T(1024)S(1)} fusion(f32[4608]{0:T(1024)S(1)} %reshape.349, s32[4096]{0:T(1024)S(1)} %broadcast_clamp_fusion.4), kind=kCustom, calls=%fused_computation.1.clone.clone.1 | custom fusion | bytes 49152 | tf_op jit(solution)/shard_map/while/body/eval_jaxpr/jit(_take)/gather | solution.py:60
  901.3 23.0 %gather_fusion = f32[4096]{0:T(1024)S(1)} fusion(f32[4608]{0:T(1024)S(1)} %reshape.349, s32[4096]{0:T(1024)S(1)} %broadcast_clamp_fusion.4), kind=kCustom, calls=%fused_computation.1.clone.clone.1 | custom fusion | bytes 49152 | tf_op jit(solution)/shard_map/while/body/eval_jaxpr/jit(_take)/gather | solution.py:60
  933.7 23.0 %gather_fusion = f32[4096]{0:T(1024)S(1)} fusion(f32[4608]{0:T(1024)S(1)} %reshape.349, s32[4096]{0:T(1024)S(1)} %broadcast_clamp_fusion.4), kind=kCustom, calls=%fused_computation.1.clone.clone.1 | custom fusion | bytes 49152 | tf_op jit(solution)/shard_map/while/body/eval_jaxpr/jit(_take)/gather | solution.py:60
  966.0 23.0 %gather_fusion = f32[4096]{0:T(1024)S(1)} fusion(f32[4608]{0:T(1024)S(1)} %reshape.349, s32[4096]{0:T(1024)S(1)} %broadcast_clamp_fusion.4), kind=kCustom, calls=%fused_computation.1.clone.clone.1 | custom fusion | bytes 49152 | tf_op jit(solution)/shard_map/while/body/eval_jaxpr/jit(_take)/gather | solution.py:60
  998.3 23.0 %gather_fusion = f32[4096]{0:T(1024)S(1)} fusion(f32[4608]{0:T(1024)S(1)} %reshape.349, s32[4096]{0:T(1024)S(1)} %broadcast_clamp_fusion.4), kind=kCustom, calls=%fused_computation.1.clone.clone.1 | custom fusion | bytes 49152 | tf_op jit(solution)/shard_map/while/body/eval_jaxpr/jit(_take)/gather | solution.py:60
  1030.6 23.0 %gather_fusion = f32[4096]{0:T(1024)S(1)} fusion(f32[4608]{0:T(1024)S(1)} %reshape.349, s32[4096]{0:T(1024)S(1)} %broadcast_clamp_fusion.4), kind=kCustom, calls=%fused_computation.1.clone.clone.1 | custom fusion | bytes 49152 | tf_op jit(solution)/shard_map/while/body/eval_jaxpr/jit(_take)/gather | solution.py:60
  1063.0 23.0 %gather_fusion = f32[4096]{0:T(1024)S(1)} fusion(f32[4608]{0:T(1024)S(1)} %reshape.349, s32[4096]{0:T(1024)S(1)} %broadcast_clamp_fusion.4), kind=kCustom, calls=%fused_computation.1.clone.clone.1 | custom fusion | bytes 49152 | tf_op jit(solution)/shard_map/while/body/eval_jaxpr/jit(_take)/gather | solution.py:60
  1118.5 180.5 %gather_fusion.4 = f32[32768]{0:T(1024)S(1)} fusion(f32[4096]{0:T(1024)S(1)} %bitcast.65, s32[32768]{0:T(1024)S(1)} %broadcast_clamp_fusion.1), kind=kCustom, calls=%fused_computation.2.clone | custom fusion | bytes 393216 | tf_op jit(solution)/shard_map/jit(_take)/gather | solution.py:67
  1308.8 213.2 %scatter_custom_fusion.4 = f32[4096]{0:T(1024)S(1)} fusion(s32[32768]{0:T(1024)S(1)} %bitcast.81, f32[32768]{0:T(1024)S(1)} %bitcast.86, f32[]{:T(128)S(6)} %convert_element_type.3), kind=kCustom, calls=%fused_computation.79 | custom fusion | flops 32768 | bytes 16388 | tf_op jit(solution)/shard_map/scatter-add | solution.py:66
  1527.3 213.2 %scatter_custom_fusion.3 = f32[4096]{0:T(1024)S(1)} fusion(s32[32768]{0:T(1024)S(1)} %bitcast.82, f32[32768]{0:T(1024)S(1)} %bitcast.84, f32[]{:T(128)} %constant.102.clone.1), kind=kCustom, calls=%fused_computation.81 | custom fusion | flops 32768 | bytes 16388 | tf_op jit(solution)/shard_map/scatter-add | solution.py:73
  (362 shorter events, 304.8 us)
Async XLA Ops:
  0.7 12.5 collective-permute-start.2
  2.4 10.8 collective-permute-start.3
  199.7 37.4 %all-to-all-start = ((f32[128,1,4096]{2,1,0:T(1,128)}), f32[128,1,4096]{2,1,0:T(1,128)S(1)}, u32[]{:S(2)}, u32[]{:S(2)}) async-start(f32[128,1,4096]{2,1,0:T(1,128)} %all_to_all.16), calls=%async_computation | async-start | bytes 4194304 | tf_op jit(solution)/shard_map/all_to_all | solution.py:42
  472.1 9.0 collective-permute-start.1
  504.4 9.1 collective-permute-start.1
  536.7 9.1 collective-permute-start.1
  569.0 9.1 collective-permute-start.1
  601.3 9.1 collective-permute-start.1
  633.7 9.1 collective-permute-start.1
  666.0 9.1 collective-permute-start.1
  698.3 9.1 collective-permute-start.1
  730.6 9.1 collective-permute-start.1
  763.0 9.1 collective-permute-start.1
  795.3 9.1 collective-permute-start.1
  827.6 9.1 collective-permute-start.1
  859.9 9.1 collective-permute-start.1
  892.3 9.1 collective-permute-start.1
  924.6 9.1 collective-permute-start.1
  956.9 9.1 collective-permute-start.1
  989.2 9.1 collective-permute-start.1
  1021.6 9.1 collective-permute-start.1
  1053.9 9.1 collective-permute-start.1
  1086.2 9.1 collective-permute-start.1
  1303.9 218.0 %all-to-all-start.1 = ((f32[128,1,4096]{2,1,0:T(1,128)}), f32[128,1,4096]{2,1,0:T(1,128)S(1)}, u32[]{:S(2)}, u32[]{:S(2)}) async-start(f32[128,1,4096]{2,1,0:T(1,128)} %copy.7), calls=%async_computation.1 | async-start | bytes 4194304 | tf_op jit(solution)/shard_map/all_to_all | solution.py:69
  (25 other events, 711.3 us)
where the time goes:
time: 1770 us; the launch traced here: 1740 us
  local copies, waits for them, and re-layouts  847 us (48%)
  other arithmetic  660 us (37%)
  waiting for transfers between devices  169 us (10%)
  starting transfers between devices  63.6 us (4%)
    gather x40, local copies, waits for them, and re-layouts, sweep_once(): jnp.take(extended.reshape(-1), index)  461 us
    scatter-add x1, other arithmetic, shards(): zeros_flat.at[incoming_marine_slot.reshape(-1)].add(incoming.reshape(-1))  226 us
    scatter-add x1, other arithmetic, shards(): zeros_flat.at[send_cell.reshape(-1)].add(remap_weight.reshape(-1))  213 us
    scatter-add x1, other arithmetic, shards(): zeros_flat.at[send_cell.reshape(-1)]  213 us
    gather x2, local copies, waits for them, and re-layouts, shards(): outgoing = remap_weight * jnp.take(air_flux, send_cell)  181 us
    gather x2, local copies, waits for them, and re-layouts, shards(): backward_transfers = jnp.take(linear_skin_heat, incoming_marine_slot)  181 us
    ppermute x21, waiting for transfers between devices, with_halo(): before = lax.ppermute(last, axis, up)  112 us
    ppermute x21, starting transfers between devices, with_halo(): before = lax.ppermute(last, axis, up)  39.9 us
  transfers between devices with their start and end apart: 44, of which 41 were waited for; matrix products, arithmetic and copies ran while one was open for 13% of the time, Pallas kernels for 0%

commit v1 on v0

v1 whole, which is shorter than its diff:
```python
import functools

import jax
import jax.numpy as jnp
from jax import lax
from jax.experimental import pallas as pl
from jax.experimental.pallas import tpu as pltpu
from jax.sharding import PartitionSpec as P

SPAN = 8
SWEEPS = 20
TILES = 64
ROWS = 16
COLS = 256
CELLS = ROWS * COLS
LANES = 128
BLOCKS = CELLS // LANES
MERGED = ((0, 1), (2, 4), (3, None), (5, None), (6, 7))
OWN = 24
WINDOW = 64
MESH = pl.DeviceIdType.MESH
F32 = jnp.float32
BF16 = jnp.bfloat16


def reverse_tile(x):
    row = 7 - lax.broadcasted_iota(jnp.int32, (8, LANES), 0)
    lane = LANES - 1 - lax.broadcasted_iota(jnp.int32, (8, LANES), 1)
    return jnp.take_along_axis(jnp.take_along_axis(x, row, axis=0), lane, axis=1)


def lookup(table, index):
    lane = index & (LANES - 1)
    bits = [((index >> (7 + b)) & 1) == 1 for b in range(5)]

    def pick(level, base):
        if level < 0:
            row = table[base // 2 : base // 2 + 1, (base % 2) * LANES : (base % 2 + 1) * LANES]
            return jnp.take_along_axis(jnp.broadcast_to(row, (8, LANES)), lane, axis=1)
        low = pick(level - 1, base)
        high = pick(level - 1, base + (1 << level))
        return jnp.where(bits[level], high, low)

    return pick(4, 0)


def spread(row, count):
    piece = jnp.broadcast_to(row.astype(F32), (16, LANES)).astype(BF16)
    return jnp.concatenate([piece] * (count // 16), 0)


def numbers(count):
    return lax.broadcasted_iota(jnp.int32, (count, LANES), 0).astype(F32).astype(BF16)


def scatter_sum(index, value):
    zero, one = jnp.zeros((), BF16), jnp.ones((), BF16)
    lefts, rights = [], []
    for j in range(BLOCKS):
        i, v = index(j), value(j)
        line = ((i >> 7) & 1) * 16 + (i >> 8)
        head = v.astype(BF16).astype(F32)
        here = spread(line, 32) == numbers(32)
        lefts.append(
            jnp.concatenate(
                [
                    jnp.where(here, spread(head, 32), zero),
                    jnp.where(here, spread(v - head, 32), zero),
                ],
                0,
            )
        )
        rights.append(jnp.where(spread(i & (LANES - 1), LANES) == numbers(LANES), one, zero))
    left = jnp.concatenate(lefts, 1)
    right = jnp.concatenate(rights, 1)
    return lax.dot_general(left, right, (((1,), (1,)), ((), ())), preferred_element_type=F32)


def halves(total):
    both = total[0:32] + total[32:64]
    return jnp.concatenate([both[0:16], both[16:32]], axis=1)


def kernel(
    state,
    coeff,
    vertical,
    send_cell,
    marine_slot,
    weight,
    out,
    own,
    rate,
    table,
    codes,
    weights,
    air_halo,
    merged,
    values,
    rows_out,
    rows_in,
    total,
    weight_sum,
    win_rhs,
    win_diag,
    win_code,
    load_sem,
    halo_send,
    halo_recv,
    row_send,
    row_recv,
    rhs_send,
    rhs_recv,
    win_send,
    win_recv,
):
    model = lax.axis_index("comp")
    tile = lax.axis_index("tile")

    def at(offset):
        return lax.rem(tile + offset + TILES, TILES)

    def copy_to(source, target, send, recv, comp, piece):
        return pltpu.make_async_remote_copy(
            src_ref=source,
            dst_ref=target,
            send_sem=send,
            recv_sem=recv,
            device_id=(comp, piece),
            device_id_type=MESH,
        )

    def load(source, target, k):
        return pltpu.make_async_copy(source, target, load_sem.at[k])

    def greet(partners):
        barrier = pltpu.get_barrier_semaphore()
        for comp, piece in partners:
            pl.semaphore_signal(barrier, inc=1, device_id=(comp, piece), device_id_type=MESH)
        pl.semaphore_wait(barrier, len(partners))

    def to_ocean(d):
        return copy_to(rows_out.at[d], rows_in.at[d], row_send.at[d], row_recv.at[d], 1, at(d - 4))

    def to_air(d):
        return copy_to(rows_out.at[d], rows_in.at[d], row_send.at[d], row_recv.at[d], 0, at(4 - d))

    def slab(ref, d, q):
        return ref[pl.ds(64 * q + d, 8, stride=8), :]

    @pl.when(model == 0)
    def _():
        loads = [
            load(send_cell, codes, 0),
            load(weight, weights, 1),
            load(state.at[0], own, 2),
            load(coeff.at[0], rate, 3),
        ]
        for item in loads:
            item.start()
        greet([(0, at(1)), (0, at(-1))] + [(1, at(d - 4)) for d in range(SPAN)])
        down = copy_to(
            state.at[0, pl.ds(8, 8)], air_halo.at[0], halo_send.at[0], halo_recv.at[0], 0, at(1)
        )
        up = copy_to(
            state.at[0, pl.ds(0, 8)], air_halo.at[1], halo_send.at[1], halo_recv.at[1], 0, at(-1)
        )
        down.start()
        up.start()
        for item in loads:
            item.wait()
        for m, (d, e) in enumerate(MERGED):
            for q in range(4):
                index = slab(codes, d, q)
                if e is not None:
                    index = index + reverse_tile(slab(codes, e, 3 - q))
                merged[m, 8 * q : 8 * q + 8, :] = index
        down.wait_recv()
        up.wait_recv()
        s = own[...]
        row_id = lax.broadcasted_iota(jnp.int32, (ROWS, COLS), 0)
        above = jnp.where(row_id == 0, air_halo[0, 7:8, :], pltpu.roll(s, 1, 0))
        below = jnp.where(row_id == ROWS - 1, air_halo[1, 0:1, :], pltpu.roll(s, ROWS - 1, 0))
        near = above + below + pltpu.roll(s, 1, 1) + pltpu.roll(s, COLS - 1, 1)
        table[...] = rate[...] * (s + 0.2 * (near - 4.0 * s))
        for m, (d, e) in enumerate(MERGED):
            for q in range(4):
                found = lookup(table, merged[m, 8 * q : 8 * q + 8, :])
                rows_out[d, 8 * q : 8 * q + 8, :] = slab(weights, d, q) * found
                if e is not None:
                    p = 3 - q
                    rows_out[e, 8 * p : 8 * p + 8, :] = slab(weights, e, p) * reverse_tile(found)
            to_ocean(d).start()
            if e is not None:
                to_ocean(e).start()
        for m, (d, e) in enumerate(MERGED):
            for q in range(4):
                w = slab(weights, d, q)
                if e is not None:
                    w = w + reverse_tile(slab(weights, e, 3 - q))
                values[m, 8 * q : 8 * q + 8, :] = w
        weight_sum[...] = jnp.zeros_like(weight_sum)
        total[...] = jnp.zeros_like(total)

        @pl.loop(0, len(MERGED))
        def _(m):
            weight_sum[...] += scatter_sum(
                lambda j: merged[m, j : j + 1, :], lambda j: values[m, j : j + 1, :]
            )

        for m, (d, e) in enumerate(MERGED):
            to_air(d).wait_recv()
            if e is not None:
                to_air(e).wait_recv()
            for q in range(4):
                v = slab(weights, d, q) * rows_in[d, 8 * q : 8 * q + 8, :]
                if e is not None:
                    p = 3 - q
                    v = v + reverse_tile(slab(weights, e, p) * rows_in[e, 8 * p : 8 * p + 8, :])
                values[m, 8 * q : 8 * q + 8, :] = v
            total[...] += scatter_sum(
                lambda j: merged[m, j : j + 1, :], lambda j: values[m, j : j + 1, :]
            )
        out[...] = halves(total[...]) / halves(weight_sum[...])
        down.wait_send()
        up.wait_send()
        for d in range(SPAN):
            to_ocean(d).wait_send()

    @pl.when(model == 1)
    def _():
        mine = pl.ds(OWN, ROWS)
        loads = [
            load(marine_slot, codes, 0),
            load(state.at[0], own, 1),
            load(coeff.at[0], win_diag.at[mine], 2),
            load(vertical, win_code.at[mine], 3),
        ]
        for item in loads:
            item.start()
        greet(
            [(1, at(1)), (1, at(-1)), (1, at(2)), (1, at(-2))]
            + [(0, at(4 - d)) for d in range(SPAN)]
        )

        def to_windows(source, target, send, recv):
            return [
                copy_to(
                    source(first, rows),
                    target.at[pl.ds(place, rows)],
                    send.at[k],
                    recv.at[k],
                    1,
                    at(offset),
                )
                for k, (offset, first, rows, place) in enumerate(
                    (
                        (1, 0, 16, OWN - 16),
                        (-1, 0, 16, OWN + 16),
                        (2, 8, 8, OWN - 24),
                        (-2, 0, 8, OWN + 32),
                    )
                )
            ]

        ahead = to_windows(
            lambda first, rows: coeff.at[0, pl.ds(first, rows)],
            win_diag,
            win_send.at[0],
            win_recv.at[0],
        ) + to_windows(
            lambda first, rows: vertical.at[pl.ds(first, rows)],
            win_code,
            win_send.at[1],
            win_recv.at[1],
        )
        for item in ahead:
            item.start()
        for item in loads:
            item.wait()
        for item in ahead:
            item.wait_recv()
        total[...] = jnp.zeros_like(total)

        @pl.loop(0, SPAN)
        def _(d):
            to_ocean(d).wait_recv()
            total[...] += scatter_sum(
                lambda j: codes[pl.ds(8 * j + d, 1), :], lambda j: rows_in[d, j : j + 1, :]
            )

        source = halves(total[...])
        win_rhs[mine, :] = source + own[...]
        sides = to_windows(
            lambda first, rows: win_rhs.at[pl.ds(OWN + first, rows)], win_rhs, rhs_send, rhs_recv
        )
        for item in sides:
            item.start()
        for item in sides:
            item.wait_recv()

        def sweeps(eta, count, margin):
            rows = WINDOW - 2 * margin
            part = pl.ds(margin, rows)
            first = eta[margin_of(eta, rows) : margin_of(eta, rows) + rows]
            code = win_code[part, :]
            far = code >= 3
            side = code - jnp.where(far, 3, 0)
            from_up = pltpu.roll(side, rows - 1, 0)
            from_down = pltpu.roll(side, 1, 0)
            scale = 1.0 / (win_diag[part, :] + 3.0)
            rhs = win_rhs[part, :]

            def one(_, x):
                left = pltpu.roll(x, 1, 1)
                right = pltpu.roll(x, COLS - 1, 1)
                up = jnp.where(from_up == 0, left, jnp.where(from_up == 1, x, right))
                down = jnp.where(from_down == 0, left, jnp.where(from_down == 1, x, right))
                third = jnp.where(far, pltpu.roll(down, rows - 1, 0), pltpu.roll(up, 1, 0))
                return (rhs + (left + right + third)) * scale

            return lax.fori_loop(0, count, one, first)

        def margin_of(x, rows):
            return (x.shape[0] - rows) // 2

        eta = win_rhs[...] / (win_diag[...] + 3.0)
        eta = sweeps(eta, 3, 0)
        eta = sweeps(eta, 8, 8)
        eta = sweeps(eta, 8, 16)
        eta = eta[8:24]
        out[...] = eta
        table[...] = own[...] + 0.5 * eta - 0.25 * source
        for d in range(SPAN):
            for q in range(4):
                rows_out[d, 8 * q : 8 * q + 8, :] = lookup(table, slab(codes, d, q))
            to_air(d).start()
        for item in ahead + sides:
            item.wait_send()
        for d in range(SPAN):
            to_air(d).wait_send()


def shards(state, coeff, vertical, send_cell, incoming_marine_slot, remap_weight):
    def blocks(x):
        return x.reshape(SPAN, BLOCKS, LANES).transpose(1, 0, 2).reshape(SPAN * BLOCKS, LANES)

    anywhere = pl.BlockSpec(memory_space=pl.ANY)
    grid = pltpu.VMEM((ROWS, COLS), F32)
    dma = pltpu.SemaphoreType.DMA
    result = pl.pallas_call(
        kernel,
        out_shape=jax.ShapeDtypeStruct((ROWS, COLS), F32),
        in_specs=[anywhere] * 6,
        out_specs=pl.BlockSpec(memory_space=pltpu.VMEM),
        scratch_shapes=[
            grid,
            grid,
            grid,
            pltpu.VMEM((SPAN * BLOCKS, LANES), jnp.int32),
            pltpu.VMEM((SPAN * BLOCKS, LANES), F32),
            pltpu.VMEM((2, 8, COLS), F32),
            pltpu.VMEM((len(MERGED), BLOCKS, LANES), jnp.int32),
            pltpu.VMEM((len(MERGED), BLOCKS, LANES), F32),
            pltpu.VMEM((SPAN, BLOCKS, LANES), F32),
            pltpu.VMEM((SPAN, BLOCKS, LANES), F32),
            pltpu.VMEM((64, LANES), F32),
            pltpu.VMEM((64, LANES), F32),
            pltpu.VMEM((WINDOW, COLS), F32),
            pltpu.VMEM((WINDOW, COLS), F32),
            pltpu.VMEM((WINDOW, COLS), jnp.int32),
            dma((4,)),
            dma((2,)),
            dma((2,)),
            dma((SPAN,)),
            dma((SPAN,)),
            dma((4,)),
            dma((4,)),
            dma((2, 4)),
            dma((2, 4)),
        ],
        compiler_params=pltpu.CompilerParams(
            collective_id=0, has_side_effects=True, vmem_limit_bytes=40 << 20
        ),
    )(
        state,
        coeff,
        vertical,
        blocks(send_cell),
        blocks(incoming_marine_slot),
        blocks(remap_weight),
    )
    return result[None]


def solution(mesh):
    in_specs = (
        P("comp", "tile", None),
        P("comp", "tile", None),
        P("tile", None),
        P(("comp", "tile"), None),
        P(("comp", "tile"), None),
        P(("comp", "tile"), None),
    )
    out_specs = P("comp", "tile", None)
    return jax.shard_map(shards, mesh=mesh, in_specs=in_specs, out_specs=out_specs, check_vma=False)
```

time: 1770 us -> 43.8 us (0.02); the launches traced: 1740 us -> 43.5 us
  local copies, waits for them, and re-layouts: 847 us -> 5.47 us
  other arithmetic: 660 us -> 0 us
  waiting for transfers between devices: 169 us -> 0 us
  starting transfers between devices: 63.6 us -> 0 us
  Pallas kernels: 0 us -> 38 us
    gather x46 -> x0, local copies, waits for them, and re-layouts: 826 us -> none  [the longest x40 461 us: sweep_once(): jnp.take(extended.reshape(-1), index)]
    scatter-add x3 -> x0, other arithmetic: 653 us -> none  [the longest x1 226 us: shards(): zeros_flat.at[incoming_marine_slot.reshape(-1)].add(incoming.reshape(-1))]
    ppermute x42 -> x0, waiting for transfers between devices: 139 us -> none  [the longest x21 112 us: with_halo(): before = lax.ppermute(last, axis, up)]
    ppermute x42 -> x0, starting transfers between devices: 51.7 us -> none  [the longest x21 39.9 us: with_halo(): before = lax.ppermute(last, axis, up)]
    pallas_call x0 -> x1, Pallas kernels: none -> 38 us  [shards(): pl.pallas_call(kernel, out_shape=jax.ShapeDtypeStruct((ROWS, COLS), F32),...]
    all_to_all x2 -> x0, waiting for transfers between devices: 29.7 us -> none  [the longest x1 29.7 us: shards(): lax.all_to_all(buffer, ('comp', 'tile'), split_axis=0, concat_axis=0, til...]
  transfers between devices with their start and end apart: 44 -> 0, of which waited for: 41 -> 0; matrix products, arithmetic and copies ran while one was open for 13% -> 0% of each run, Pallas kernels for 0% -> 0%
where the time goes in v1:
time: 43.8 us; the launch traced here: 43.5 us
  Pallas kernels  38 us (87%)
  local copies, waits for them, and re-layouts  5.47 us (12%)
    pallas_call x1, Pallas kernels, shards(): pl.pallas_call(kernel, out_shape=jax.ShapeDtypeStruct((ROWS, COLS), F32),...  38 us
    unnamed x13, local copies, waits for them, and re-layouts  5.47 us

profile of v1, /device:TPU:0, one launch (start us, length us, event | category | flops | bytes accessed | tf_op | source)
XLA Modules:
  0.0 43.5 jit_solution(6058139100033460030)
XLA Ops:
  0.0 0.0 copy-start
  0.0 0.9 %copy-done = s32[8,4096]{1,0:T(8,128)S(1)} copy-done((s32[8,4096]{1,0:T(8,128)S(1)}, s32[8,4096]{1,0:T(8,128)}, u32[]{:S(2)}) %copy-start) | copy-done | bytes 131096
  0.9 0.0 copy-start.1
  0.9 0.9 %copy-done.1 = s32[8,4096]{1,0:T(8,128)S(1)} copy-done((s32[8,4096]{1,0:T(8,128)S(1)}, s32[8,4096]{1,0:T(8,128)}, u32[]{:S(2)}) %copy-start.1) | copy-done | bytes 131096
  1.8 0.0 copy-start.2
  1.8 0.9 %copy-done.2 = f32[8,4096]{1,0:T(8,128)S(1)} copy-done((f32[8,4096]{1,0:T(8,128)S(1)}, f32[8,4096]{1,0:T(8,128)}, u32[]{:S(2)}) %copy-start.2) | copy-done | bytes 131096
  2.7 0.0 copy-start.3
  2.7 0.7 %copy-done.3 = f32[1,16,256]{2,1,0:T(8,128)S(1)} copy-done((f32[1,16,256]{2,1,0:T(8,128)S(1)}, f32[1,16,256]{2,1,0:T(8,128)}, u32[]{:S(2)}) %copy-start.3) | copy-done | bytes 16408
  3.4 0.0 copy-start.4
  3.4 0.7 %copy-done.4 = f32[1,16,256]{2,1,0:T(8,128)S(1)} copy-done((f32[1,16,256]{2,1,0:T(8,128)S(1)}, f32[1,16,256]{2,1,0:T(8,128)}, u32[]{:S(2)}) %copy-start.4) | copy-done | bytes 16408
  4.2 0.0 copy-start.5
  4.2 0.7 %copy-done.5 = s32[16,256]{1,0:T(8,128)S(1)} copy-done((s32[16,256]{1,0:T(8,128)S(1)}, s32[16,256]{1,0:T(8,128)}, u32[]{:S(2)}) %copy-start.5) | copy-done | bytes 16408
  4.9 38.0 %shard_map.64 = f32[16,256]{1,0:T(8,128)S(1)} custom-call(f32[1,16,256]{2,1,0:T(8,128)S(1)} %copy-done.3, f32[1,16,256]{2,1,0:T(8,128)S(1)} %copy-done.4, s32[16,256]{1,0:T(8,128)S(1)} %copy-done.5, s32[256,128]{1,0:T(8,128)S(1)} %bitcast.16, s32[256,128]{1,0:T(8,128)S(1)} %bitcast.17, f32[256,128]{1,0:T(8,128)S(1)} %bitcast.18), custom_call_target="tpu_custom_call" | custom-call | tf_op jit(solution)/shard_map/pallas_call | solution.py:351
  42.9 0.6 %copy.8 = f32[1,16,256]{2,1,0:T(8,128)} copy(f32[1,16,256]{2,1,0:T(8,128)S(1)} %bitcast.19) | data formatting | bytes 32768
Async XLA Ops:
  0.0 0.9 %copy-start = (s32[8,4096]{1,0:T(8,128)S(1)}, s32[8,4096]{1,0:T(8,128)}, u32[]{:S(2)}) copy-start(s32[8,4096]{1,0:T(8,128)} %param.9) | copy-start | bytes 393220
  0.9 0.9 %copy-start.1 = (s32[8,4096]{1,0:T(8,128)S(1)}, s32[8,4096]{1,0:T(8,128)}, u32[]{:S(2)}) copy-start(s32[8,4096]{1,0:T(8,128)} %param.10) | copy-start | bytes 393220
  1.8 0.9 %copy-start.2 = (f32[8,4096]{1,0:T(8,128)S(1)}, f32[8,4096]{1,0:T(8,128)}, u32[]{:S(2)}) copy-start(f32[8,4096]{1,0:T(8,128)} %param.11) | copy-start | bytes 393220
  2.7 0.7 %copy-start.3 = (f32[1,16,256]{2,1,0:T(8,128)S(1)}, f32[1,16,256]{2,1,0:T(8,128)}, u32[]{:S(2)}) copy-start(f32[1,16,256]{2,1,0:T(8,128)} %state.1) | copy-start | bytes 49156
  3.4 0.7 %copy-start.4 = (f32[1,16,256]{2,1,0:T(8,128)S(1)}, f32[1,16,256]{2,1,0:T(8,128)}, u32[]{:S(2)}) copy-start(f32[1,16,256]{2,1,0:T(8,128)} %coeff.1) | copy-start | bytes 49156
  4.2 0.7 %copy-start.5 = (s32[16,256]{1,0:T(8,128)S(1)}, s32[16,256]{1,0:T(8,128)}, u32[]{:S(2)}) copy-start(s32[16,256]{1,0:T(8,128)} %vertical.1) | copy-start | bytes 49156

commit v2 on v1

--- a/solution.py
+++ b/solution.py
@@ -345,7 +345,7 @@
     def blocks(x):
         return x.reshape(SPAN, BLOCKS, LANES).transpose(1, 0, 2).reshape(SPAN * BLOCKS, LANES)
 
-    anywhere = pl.BlockSpec(memory_space=pl.ANY)
+    anywhere = pl.BlockSpec(memory_space=pltpu.HBM)
     grid = pltpu.VMEM((ROWS, COLS), F32)
     dma = pltpu.SemaphoreType.DMA
     result = pl.pallas_call(
@@ -383,12 +383,17 @@
             collective_id=0, has_side_effects=True, vmem_limit_bytes=40 << 20
         ),
     )(
-        state,
-        coeff,
-        vertical,
-        blocks(send_cell),
-        blocks(incoming_marine_slot),
-        blocks(remap_weight),
+        *(
+            pltpu.with_memory_space_constraint(x, pltpu.HBM)
+            for x in (
+                state,
+                coeff,
+                vertical,
+                blocks(send_cell),
+                blocks(incoming_marine_slot),
+                blocks(remap_weight),
+            )
+        )
     )
     return result[None]
 

time: 43.8 us -> 38.6 us (0.88)
  local copies, waits for them, and re-layouts: 5.47 us -> 0.61 us
    unnamed x13 -> x1, local copies, waits for them, and re-layouts: 5.47 us -> 0.61 us
where the time goes in v2:
time: 38.6 us; the launch traced here: 38.5 us
  Pallas kernels  37.9 us (98%)
  local copies, waits for them, and re-layouts  0.61 us (2%)
    pallas_call x1, Pallas kernels, shards(): pl.pallas_call(kernel, out_shape=jax.ShapeDtypeStruct((ROWS, COLS), F32),...  37.9 us

profile of v2, /device:TPU:0, one launch (start us, length us, event | category | flops | bytes accessed | tf_op | source)
XLA Modules:
  0.0 38.5 jit_solution(3431428424167490046)
XLA Ops:
  0.0 37.9 %shard_map.64 = f32[16,256]{1,0:T(8,128)S(1)} custom-call(f32[1,16,256]{2,1,0:T(8,128)} %state.1, f32[1,16,256]{2,1,0:T(8,128)} %coeff.1, s32[16,256]{1,0:T(8,128)} %vertical.1, s32[256,128]{1,0:T(8,128)} %bitcast.17, s32[256,128]{1,0:T(8,128)} %bitcast.18, f32[256,128]{1,0:T(8,128)} %bitcast.19), custom_call_target="tpu_custom_call" | custom-call | tf_op jit(solution)/shard_map/pallas_call | solution.py:351
  37.9 0.6 %copy.8 = f32[1,16,256]{2,1,0:T(8,128)} copy(f32[1,16,256]{2,1,0:T(8,128)S(1)} %bitcast.16) | data formatting | bytes 32768

commit v3 on v2

--- a/solution.py
+++ b/solution.py
@@ -42,6 +42,18 @@
         return jnp.where(bits[level], high, low)
 
     return pick(4, 0)
+
+
+def edge_lookup(rows, column):
+    lane = column & (LANES - 1)
+    right = ((column >> 7) & 1) == 1
+
+    def read(k):
+        return jnp.take_along_axis(jnp.broadcast_to(rows[k], (8, LANES)), lane, axis=1)
+
+    return jnp.where(
+        column >= COLS, jnp.where(right, read(3), read(2)), jnp.where(right, read(1), read(0))
+    )
 
 
 def spread(row, count):
@@ -94,7 +106,8 @@
     table,
     codes,
     weights,
-    air_halo,
+    edge_out,
+    edges,
     merged,
     values,
     rows_out,
@@ -105,8 +118,8 @@
     win_diag,
     win_code,
     load_sem,
-    halo_send,
-    halo_recv,
+    edge_send,
+    edge_recv,
     row_send,
     row_recv,
     rhs_send,
@@ -116,6 +129,7 @@
 ):
     model = lax.axis_index("comp")
     tile = lax.axis_index("tile")
+    turn = lax.rem(tile, 4) // 2
 
     def at(offset):
         return lax.rem(tile + offset + TILES, TILES)
@@ -134,16 +148,39 @@
         return pltpu.make_async_copy(source, target, load_sem.at[k])
 
     def greet(partners):
-        barrier = pltpu.get_barrier_semaphore()
         for comp, piece in partners:
-            pl.semaphore_signal(barrier, inc=1, device_id=(comp, piece), device_id_type=MESH)
-        pl.semaphore_wait(barrier, len(partners))
+            pl.semaphore_signal(
+                pltpu.get_barrier_semaphore(),
+                inc=1,
+                device_id=(comp, piece),
+                device_id_type=MESH,
+            )
+
+    def met(count):
+        pl.semaphore_wait(pltpu.get_barrier_semaphore(), count)
 
     def to_ocean(d):
         return copy_to(rows_out.at[d], rows_in.at[d], row_send.at[d], row_recv.at[d], 1, at(d - 4))
 
     def to_air(d):
-        return copy_to(rows_out.at[d], rows_in.at[d], row_send.at[d], row_recv.at[d], 0, at(4 - d))
+        first = pl.ds(0, BLOCKS)
+        return copy_to(
+            rows_out.at[d, first],
+            rows_in.at[d, first],
+            row_send.at[d],
+            row_recv.at[d],
+            0,
+            at(4 - d),
+        )
+
+    def edge_to_ocean(e):
+        return copy_to(edge_out, edges.at[e], edge_send.at[e], edge_recv.at[e], 1, at(4 - e))
+
+    def behind_first(i):
+        return lax.rem(11 - 6 * turn + i * (2 * turn - 1) + 8, 8)
+
+    def ahead_first(i):
+        return lax.rem(5 + 6 * turn + i * (1 - 2 * turn) + 8, 8)
 
     def slab(ref, d, q):
         return ref[pl.ds(64 * q + d, 8, stride=8), :]
@@ -151,54 +188,61 @@
     @pl.when(model == 0)
     def _():
         loads = [
+            load(state.at[0], own, 2),
+            load(coeff.at[0], rate, 3),
             load(send_cell, codes, 0),
             load(weight, weights, 1),
-            load(state.at[0], own, 2),
-            load(coeff.at[0], rate, 3),
         ]
         for item in loads:
             item.start()
-        greet([(0, at(1)), (0, at(-1))] + [(1, at(d - 4)) for d in range(SPAN)])
-        down = copy_to(
-            state.at[0, pl.ds(8, 8)], air_halo.at[0], halo_send.at[0], halo_recv.at[0], 0, at(1)
-        )
-        up = copy_to(
-            state.at[0, pl.ds(0, 8)], air_halo.at[1], halo_send.at[1], halo_recv.at[1], 0, at(-1)
-        )
-        down.start()
-        up.start()
-        for item in loads:
+        greet([(1, at(4 - e)) for e in range(SPAN + 2)])
+        for item in loads[:2]:
+            item.wait()
+        s = own[...]
+        for k, r in enumerate((0, ROWS - 1)):
+            for h in range(2):
+                edge_out[2 * k + h : 2 * k + h + 1, :] = own[r : r + 1, h * LANES : (h + 1) * LANES]
+        row_id = lax.broadcasted_iota(jnp.int32, (ROWS, COLS), 0)
+        above = jnp.where(row_id == 0, 0.0, pltpu.roll(s, 1, 0))
+        below = jnp.where(row_id == ROWS - 1, 0.0, pltpu.roll(s, ROWS - 1, 0))
+        near = above + below + pltpu.roll(s, 1, 1) + pltpu.roll(s, COLS - 1, 1)
+        table[...] = rate[...] * (s + 0.2 * (near - 4.0 * s))
+        side_rates = [
+            0.2 * rate[r : r + 1, h * LANES : (h + 1) * LANES] for r in (0, ROWS - 1) for h in (0, 1)
+        ]
+        for item in loads[2:]:
             item.wait()
         for m, (d, e) in enumerate(MERGED):
             for q in range(4):
-                index = slab(codes, d, q)
+                part = slice(8 * q, 8 * q + 8)
+                cell = slab(codes, d, q)
                 if e is not None:
-                    index = index + reverse_tile(slab(codes, e, 3 - q))
-                merged[m, 8 * q : 8 * q + 8, :] = index
-        down.wait_recv()
-        up.wait_recv()
-        s = own[...]
-        row_id = lax.broadcasted_iota(jnp.int32, (ROWS, COLS), 0)
-        above = jnp.where(row_id == 0, air_halo[0, 7:8, :], pltpu.roll(s, 1, 0))
-        below = jnp.where(row_id == ROWS - 1, air_halo[1, 0:1, :], pltpu.roll(s, ROWS - 1, 0))
-        near = above + below + pltpu.roll(s, 1, 1) + pltpu.roll(s, COLS - 1, 1)
-        table[...] = rate[...] * (s + 0.2 * (near - 4.0 * s))
-        for m, (d, e) in enumerate(MERGED):
-            for q in range(4):
-                found = lookup(table, merged[m, 8 * q : 8 * q + 8, :])
-                rows_out[d, 8 * q : 8 * q + 8, :] = slab(weights, d, q) * found
+                    cell = cell + reverse_tile(slab(codes, e, 3 - q))
+                merged[m, part, :] = cell
+                found = lookup(table, cell)
+                row = cell >> 8
+                column = (cell & (COLS - 1)) + jnp.where(row == ROWS - 1, COLS, 0)
+                gain = jnp.where(
+                    (row == 0) | (row == ROWS - 1), edge_lookup(side_rates, column), 0.0
+                )
+                place = column.astype(F32)
+                w = slab(weights, d, q)
+                rows_out[d, 8 * q : 8 * q + 8, :] = w * found
+                rows_out[d, 32 + 8 * q : 40 + 8 * q, :] = w * gain
+                rows_out[d, 64 + 8 * q : 72 + 8 * q, :] = place
                 if e is not None:
                     p = 3 - q
-                    rows_out[e, 8 * p : 8 * p + 8, :] = slab(weights, e, p) * reverse_tile(found)
-            to_ocean(d).start()
-            if e is not None:
-                to_ocean(e).start()
-        for m, (d, e) in enumerate(MERGED):
-            for q in range(4):
-                w = slab(weights, d, q)
-                if e is not None:
-                    w = w + reverse_tile(slab(weights, e, 3 - q))
-                values[m, 8 * q : 8 * q + 8, :] = w
+                    x = slab(weights, e, p)
+                    rows_out[e, 8 * p : 8 * p + 8, :] = x * reverse_tile(found)
+                    rows_out[e, 32 + 8 * p : 40 + 8 * p, :] = x * reverse_tile(gain)
+                    rows_out[e, 64 + 8 * p : 72 + 8 * p, :] = reverse_tile(place)
+                    w = w + reverse_tile(x)
+                values[m, part, :] = w
+        met(SPAN + 2)
+        for e in range(SPAN + 2):
+            edge_to_ocean(e).start()
+        for i in range(SPAN):
+            to_ocean(behind_first(i)).start()
         weight_sum[...] = jnp.zeros_like(weight_sum)
         total[...] = jnp.zeros_like(total)
 
@@ -208,22 +252,32 @@
                 lambda j: merged[m, j : j + 1, :], lambda j: values[m, j : j + 1, :]
             )
 
-        for m, (d, e) in enumerate(MERGED):
+        share = 1.0 / halves(weight_sum[...])
+        order = (3, 4, 1, 0, 2)
+        for m, n in zip(order, order[::-1]):
+
+            def either(x, y):
+                return x + turn * (y - x)
+
+            d = either(MERGED[m][0], MERGED[n][0])
             to_air(d).wait_recv()
-            if e is not None:
+            pair = MERGED[m][1] is not None
+            if pair:
+                e = either(MERGED[m][1], MERGED[n][1])
                 to_air(e).wait_recv()
             for q in range(4):
                 v = slab(weights, d, q) * rows_in[d, 8 * q : 8 * q + 8, :]
-                if e is not None:
+                if pair:
                     p = 3 - q
                     v = v + reverse_tile(slab(weights, e, p) * rows_in[e, 8 * p : 8 * p + 8, :])
-                values[m, 8 * q : 8 * q + 8, :] = v
+                values[0, 8 * q : 8 * q + 8, :] = v
+            which = either(m, n)
             total[...] += scatter_sum(
-                lambda j: merged[m, j : j + 1, :], lambda j: values[m, j : j + 1, :]
-            )
-        out[...] = halves(total[...]) / halves(weight_sum[...])
-        down.wait_send()
-        up.wait_send()
+                lambda j: merged[which, j : j + 1, :], lambda j: values[0, j : j + 1, :]
+            )
+        out[...] = halves(total[...]) * share
+        for e in range(SPAN + 2):
+            edge_to_ocean(e).wait_send()
         for d in range(SPAN):
             to_ocean(d).wait_send()
 
@@ -239,8 +293,8 @@
         for item in loads:
             item.start()
         greet(
-            [(1, at(1)), (1, at(-1)), (1, at(2)), (1, at(-2))]
-            + [(0, at(4 - d)) for d in range(SPAN)]
+            [(0, at(e - 4)) for e in range(SPAN + 2)]
+            + [(1, at(1)), (1, at(-1)), (1, at(2)), (1, at(-2))]
         )
 
         def to_windows(source, target, send, recv):
@@ -274,19 +328,48 @@
             win_send.at[1],
             win_recv.at[1],
         )
+        total[...] = jnp.zeros_like(total)
+        met(SPAN + 6)
         for item in ahead:
             item.start()
         for item in loads:
             item.wait()
-        for item in ahead:
-            item.wait_recv()
-        total[...] = jnp.zeros_like(total)
+
+        def edges_here(slots):
+            for e in slots:
+                edge_to_ocean(e).wait_recv()
+
+        @pl.when(turn == 0)
+        def _():
+            edges_here(range(4, 10))
+
+        @pl.when(turn == 1)
+        def _():
+            edges_here(range(0, 5))
 
         @pl.loop(0, SPAN)
-        def _(d):
+        def _(i):
+            d = behind_first(i)
+
+            @pl.when((turn == 0) & (i == 4))
+            def _():
+                edges_here(range(0, 4))
+
+            @pl.when((turn == 1) & (i == 3))
+            def _():
+                edges_here(range(5, 10))
+
             to_ocean(d).wait_recv()
+            above = edges.at[7 - d]
+            below = edges.at[9 - d]
+            sides = [above[2:3, :], above[3:4, :], below[0:1, :], below[1:2, :]]
+            for q in range(4):
+                column = rows_in[d, 64 + 8 * q : 72 + 8 * q, :].astype(jnp.int32)
+                values[0, 8 * q : 8 * q + 8, :] = rows_in[d, 8 * q : 8 * q + 8, :] + rows_in[
+                    d, 32 + 8 * q : 40 + 8 * q, :
+                ] * edge_lookup(sides, column)
             total[...] += scatter_sum(
-                lambda j: codes[pl.ds(8 * j + d, 1), :], lambda j: rows_in[d, j : j + 1, :]
+                lambda j: codes[pl.ds(8 * j + d, 1), :], lambda j: values[0, j : j + 1, :]
             )
 
         source = halves(total[...])
@@ -296,13 +379,13 @@
         )
         for item in sides:
             item.start()
-        for item in sides:
+        for item in ahead + sides:
             item.wait_recv()
 
         def sweeps(eta, count, margin):
             rows = WINDOW - 2 * margin
             part = pl.ds(margin, rows)
-            first = eta[margin_of(eta, rows) : margin_of(eta, rows) + rows]
+            skip = (eta.shape[0] - rows) // 2
             code = win_code[part, :]
             far = code >= 3
             side = code - jnp.where(far, 3, 0)
@@ -319,22 +402,23 @@
                 third = jnp.where(far, pltpu.roll(down, rows - 1, 0), pltpu.roll(up, 1, 0))
                 return (rhs + (left + right + third)) * scale
 
-            return lax.fori_loop(0, count, one, first)
-
-        def margin_of(x, rows):
-            return (x.shape[0] - rows) // 2
+            return lax.fori_loop(0, count, one, eta[skip : skip + rows])
 
         eta = win_rhs[...] / (win_diag[...] + 3.0)
         eta = sweeps(eta, 3, 0)
         eta = sweeps(eta, 8, 8)
         eta = sweeps(eta, 8, 16)
         eta = eta[8:24]
-        out[...] = eta
         table[...] = own[...] + 0.5 * eta - 0.25 * source
-        for d in range(SPAN):
+
+        @pl.loop(0, SPAN)
+        def _(i):
+            d = ahead_first(i)
             for q in range(4):
                 rows_out[d, 8 * q : 8 * q + 8, :] = lookup(table, slab(codes, d, q))
             to_air(d).start()
+
+        out[...] = eta
         for item in ahead + sides:
             item.wait_send()
         for d in range(SPAN):
@@ -359,19 +443,20 @@
             grid,
             pltpu.VMEM((SPAN * BLOCKS, LANES), jnp.int32),
             pltpu.VMEM((SPAN * BLOCKS, LANES), F32),
-            pltpu.VMEM((2, 8, COLS), F32),
+            pltpu.VMEM((8, LANES), F32),
+            pltpu.VMEM((SPAN + 2, 8, LANES), F32),
             pltpu.VMEM((len(MERGED), BLOCKS, LANES), jnp.int32),
             pltpu.VMEM((len(MERGED), BLOCKS, LANES), F32),
-            pltpu.VMEM((SPAN, BLOCKS, LANES), F32),
-            pltpu.VMEM((SPAN, BLOCKS, LANES), F32),
+            pltpu.VMEM((SPAN, 3 * BLOCKS, LANES), F32),
+            pltpu.VMEM((SPAN, 3 * BLOCKS, LANES), F32),
             pltpu.VMEM((64, LANES), F32),
             pltpu.VMEM((64, LANES), F32),
             pltpu.VMEM((WINDOW, COLS), F32),
             pltpu.VMEM((WINDOW, COLS), F32),
             pltpu.VMEM((WINDOW, COLS), jnp.int32),
             dma((4,)),
-            dma((2,)),
-            dma((2,)),
+            dma((SPAN + 2,)),
+            dma((SPAN + 2,)),
             dma((SPAN,)),
             dma((SPAN,)),
             dma((4,)),

time: 38.6 us -> 32.9 us (0.85)
  Pallas kernels: 37.9 us -> 32.2 us
    pallas_call x1, Pallas kernels: 37.9 us -> 32.2 us  [shards(): pl.pallas_call(kernel, out_shape=jax.ShapeDtypeStruct((ROWS, COLS), F32),...]
where the time goes in v3:
time: 32.9 us; the launch traced here: 32.8 us
  Pallas kernels  32.2 us (98%)
  local copies, waits for them, and re-layouts  0.61 us (2%)
    pallas_call x1, Pallas kernels, shards(): pl.pallas_call(kernel, out_shape=jax.ShapeDtypeStruct((ROWS, COLS), F32),...  32.2 us

profile of v3, /device:TPU:0, one launch (start us, length us, event | category | flops | bytes accessed | tf_op | source)
XLA Modules:
  0.0 32.8 jit_solution(16612852050073109719)
XLA Ops:
  0.0 32.2 %shard_map.64 = f32[16,256]{1,0:T(8,128)S(1)} custom-call(f32[1,16,256]{2,1,0:T(8,128)} %state.1, f32[1,16,256]{2,1,0:T(8,128)} %coeff.1, s32[16,256]{1,0:T(8,128)} %vertical.1, s32[256,128]{1,0:T(8,128)} %bitcast.17, s32[256,128]{1,0:T(8,128)} %bitcast.18, f32[256,128]{1,0:T(8,128)} %bitcast.19), custom_call_target="tpu_custom_call" | custom-call | tf_op jit(solution)/shard_map/pallas_call | solution.py:435
  32.2 0.6 %copy.8 = f32[1,16,256]{2,1,0:T(8,128)} copy(f32[1,16,256]{2,1,0:T(8,128)S(1)} %bitcast.16) | data formatting | bytes 32768

commit v4 on v3

--- a/solution.py
+++ b/solution.py
@@ -17,7 +17,10 @@
 BLOCKS = CELLS // LANES
 MERGED = ((0, 1), (2, 4), (3, None), (5, None), (6, 7))
 OWN = 24
+INNER = 2 * COLS
 WINDOW = 64
+FIRST = 4
+DEPTH = 7
 MESH = pl.DeviceIdType.MESH
 F32 = jnp.float32
 BF16 = jnp.bfloat16
@@ -29,9 +32,17 @@
     return jnp.take_along_axis(jnp.take_along_axis(x, row, axis=0), lane, axis=1)
 
 
-def lookup(table, index):
-    lane = index & (LANES - 1)
-    bits = [((index >> (7 + b)) & 1) == 1 for b in range(5)]
+def by_half(cell):
+    return (cell >> 7) & 1, cell & (LANES - 1)
+
+
+def by_parity(cell):
+    return cell & 1, (cell >> 1) & (LANES - 1)
+
+
+def lookup(table, index, split=by_half):
+    half, lane = split(index)
+    bits = [half == 1] + [((index >> (8 + b)) & 1) == 1 for b in range(4)]
 
     def pick(level, base):
         if level < 0:
@@ -65,12 +76,13 @@
     return lax.broadcasted_iota(jnp.int32, (count, LANES), 0).astype(F32).astype(BF16)
 
 
-def scatter_sum(index, value):
+def scatter_sum(index, value, split=by_half):
     zero, one = jnp.zeros((), BF16), jnp.ones((), BF16)
     lefts, rights = [], []
     for j in range(BLOCKS):
         i, v = index(j), value(j)
-        line = ((i >> 7) & 1) * 16 + (i >> 8)
+        half, lane = split(i)
+        line = half * 16 + (i >> 8)
         head = v.astype(BF16).astype(F32)
         here = spread(line, 32) == numbers(32)
         lefts.append(
@@ -82,10 +94,31 @@
                 0,
             )
         )
-        rights.append(jnp.where(spread(i & (LANES - 1), LANES) == numbers(LANES), one, zero))
+        rights.append(jnp.where(spread(lane, LANES) == numbers(LANES), one, zero))
     left = jnp.concatenate(lefts, 1)
     right = jnp.concatenate(rights, 1)
     return lax.dot_general(left, right, (((1,), (1,)), ((), ())), preferred_element_type=F32)
+
+
+def even_odd(ref, first):
+    parts = [ref[first : first + 8, h * LANES : (h + 1) * LANES] for h in (0, 1)]
+    lane = lax.broadcasted_iota(jnp.int32, (8, LANES), 1)
+    found = []
+    for odd in (0, 1):
+        place = (2 * lane + odd) & (LANES - 1)
+        left, right = (jnp.take_along_axis(x, place, axis=1) for x in parts)
+        found.append(jnp.where(lane < LANES // 2, left, right))
+    return found
+
+
+def interleaved(even, odd):
+    lane = lax.broadcasted_iota(jnp.int32, (8, LANES), 1)
+    parts = []
+    for h in (0, 1):
+        place = (lane >> 1) + h * (LANES // 2)
+        x, y = (jnp.take_along_axis(part, place, axis=1) for part in (even, odd))
+        parts.append(jnp.where((lane & 1) == 0, x, y))
+    return jnp.concatenate(parts, axis=1)
 
 
 def halves(total):
@@ -117,6 +150,12 @@
     win_rhs,
     win_diag,
     win_code,
+    scale,
+    turns,
+    tile_first,
+    tile_scale,
+    tile_far,
+    tile_side,
     load_sem,
     edge_send,
     edge_recv,
@@ -129,7 +168,9 @@
 ):
     model = lax.axis_index("comp")
     tile = lax.axis_index("tile")
-    turn = lax.rem(tile, 4) // 2
+    line = lax.rem(tile, 16) // 4
+    is_first = (3 - line) // 3
+    is_last = line // 3
 
     def at(offset):
         return lax.rem(tile + offset + TILES, TILES)
@@ -176,11 +217,22 @@
     def edge_to_ocean(e):
         return copy_to(edge_out, edges.at[e], edge_send.at[e], edge_recv.at[e], 1, at(4 - e))
 
-    def behind_first(i):
-        return lax.rem(11 - 6 * turn + i * (2 * turn - 1) + 8, 8)
-
-    def ahead_first(i):
-        return lax.rem(5 + 6 * turn + i * (1 - 2 * turn) + 8, 8)
+    def in_order(first, middle, last):
+        first, middle, last = (
+            sum(d * 8**i for i, d in enumerate(order)) for order in (first, middle, last)
+        )
+        return middle + is_first * (first - middle) + is_last * (last - middle)
+
+    row_order = in_order(
+        (3, 2, 1, 0, 4, 5, 6, 7), (3, 5, 2, 6, 1, 7, 0, 4), (5, 6, 7, 4, 0, 3, 2, 1)
+    )
+
+    def for_each(order, body):
+        def step(i, rest):
+            body(i, lax.rem(rest, 8))
+            return rest // 8
+
+        lax.fori_loop(0, SPAN, step, order)
 
     def slab(ref, d, q):
         return ref[pl.ds(64 * q + d, 8, stride=8), :]
@@ -199,14 +251,14 @@
         for item in loads[:2]:
             item.wait()
         s = own[...]
-        for k, r in enumerate((0, ROWS - 1)):
+        near = s + pltpu.roll(s, 1, 1) + pltpu.roll(s, COLS - 1, 1)
+        above, below = pltpu.roll(s, 1, 0), pltpu.roll(s, ROWS - 1, 0)
+        table[...] = 0.2 * rate[...] * (near + above + below)
+        for k, (r, part) in enumerate(((0, near + below), (ROWS - 1, near + above))):
             for h in range(2):
-                edge_out[2 * k + h : 2 * k + h + 1, :] = own[r : r + 1, h * LANES : (h + 1) * LANES]
-        row_id = lax.broadcasted_iota(jnp.int32, (ROWS, COLS), 0)
-        above = jnp.where(row_id == 0, 0.0, pltpu.roll(s, 1, 0))
-        below = jnp.where(row_id == ROWS - 1, 0.0, pltpu.roll(s, ROWS - 1, 0))
-        near = above + below + pltpu.roll(s, 1, 1) + pltpu.roll(s, COLS - 1, 1)
-        table[...] = rate[...] * (s + 0.2 * (near - 4.0 * s))
+                at_side = slice(h * LANES, (h + 1) * LANES)
+                edge_out[2 * k + h : 2 * k + h + 1, :] = s[r : r + 1, at_side]
+                edge_out[4 + 2 * k + h : 5 + 2 * k + h, :] = part[r : r + 1, at_side]
         side_rates = [
             0.2 * rate[r : r + 1, h * LANES : (h + 1) * LANES] for r in (0, ROWS - 1) for h in (0, 1)
         ]
@@ -219,30 +271,25 @@
                 if e is not None:
                     cell = cell + reverse_tile(slab(codes, e, 3 - q))
                 merged[m, part, :] = cell
-                found = lookup(table, cell)
                 row = cell >> 8
                 column = (cell & (COLS - 1)) + jnp.where(row == ROWS - 1, COLS, 0)
-                gain = jnp.where(
-                    (row == 0) | (row == ROWS - 1), edge_lookup(side_rates, column), 0.0
-                )
-                place = column.astype(F32)
+                outer = (row == 0) | (row == ROWS - 1)
+                found = jnp.where(outer, edge_lookup(side_rates, column), lookup(table, cell))
+                place = jnp.where(outer, column, INNER).astype(F32)
                 w = slab(weights, d, q)
-                rows_out[d, 8 * q : 8 * q + 8, :] = w * found
-                rows_out[d, 32 + 8 * q : 40 + 8 * q, :] = w * gain
-                rows_out[d, 64 + 8 * q : 72 + 8 * q, :] = place
+                rows_out[d, part, :] = w * found
+                rows_out[d, 32 + 8 * q : 40 + 8 * q, :] = place
                 if e is not None:
                     p = 3 - q
                     x = slab(weights, e, p)
                     rows_out[e, 8 * p : 8 * p + 8, :] = x * reverse_tile(found)
-                    rows_out[e, 32 + 8 * p : 40 + 8 * p, :] = x * reverse_tile(gain)
-                    rows_out[e, 64 + 8 * p : 72 + 8 * p, :] = reverse_tile(place)
+                    rows_out[e, 32 + 8 * p : 40 + 8 * p, :] = reverse_tile(place)
                     w = w + reverse_tile(x)
                 values[m, part, :] = w
         met(SPAN + 2)
         for e in range(SPAN + 2):
             edge_to_ocean(e).start()
-        for i in range(SPAN):
-            to_ocean(behind_first(i)).start()
+        for_each(row_order, lambda i, d: to_ocean(d).start())
         weight_sum[...] = jnp.zeros_like(weight_sum)
         total[...] = jnp.zeros_like(total)
 
@@ -253,11 +300,11 @@
             )
 
         share = 1.0 / halves(weight_sum[...])
-        order = (3, 4, 1, 0, 2)
+        order = (2, 0, 1, 4, 3)
         for m, n in zip(order, order[::-1]):
 
             def either(x, y):
-                return x + turn * (y - x)
+                return x + is_first * (y - x)
 
             d = either(MERGED[m][0], MERGED[n][0])
             to_air(d).wait_recv()
@@ -299,14 +346,7 @@
 
         def to_windows(source, target, send, recv):
             return [
-                copy_to(
-                    source(first, rows),
-                    target.at[pl.ds(place, rows)],
-                    send.at[k],
-                    recv.at[k],
-                    1,
-                    at(offset),
-                )
+                copy_to(source(first, rows), target(place, rows), send.at[k], recv.at[k], 1, at(offset))
                 for k, (offset, first, rows, place) in enumerate(
                     (
                         (1, 0, 16, OWN - 16),
@@ -319,12 +359,12 @@
 
         ahead = to_windows(
             lambda first, rows: coeff.at[0, pl.ds(first, rows)],
-            win_diag,
+            lambda place, rows: win_diag.at[pl.ds(place, rows)],
             win_send.at[0],
             win_recv.at[0],
         ) + to_windows(
             lambda first, rows: vertical.at[pl.ds(first, rows)],
-            win_code,
+            lambda place, rows: win_code.at[pl.ds(place, rows)],
             win_send.at[1],
             win_recv.at[1],
         )
@@ -339,86 +379,126 @@
             for e in slots:
                 edge_to_ocean(e).wait_recv()
 
-        @pl.when(turn == 0)
+        @pl.when(is_last == 0)
         def _():
             edges_here(range(4, 10))
 
-        @pl.when(turn == 1)
+        @pl.when(is_first == 0)
         def _():
-            edges_here(range(0, 5))
-
-        @pl.loop(0, SPAN)
-        def _(i):
-            d = behind_first(i)
-
-            @pl.when((turn == 0) & (i == 4))
+            edges_here(range(0, 4))
+
+        @pl.when(is_last == 1)
+        def _():
+            edges_here(range(4, 5))
+
+        def take(i, rest):
+            @pl.when((is_first == 1) & (i == 2))
             def _():
                 edges_here(range(0, 4))
 
-            @pl.when((turn == 1) & (i == 3))
+            @pl.when((is_last == 1) & (i == 1))
             def _():
                 edges_here(range(5, 10))
 
-            to_ocean(d).wait_recv()
-            above = edges.at[7 - d]
-            below = edges.at[9 - d]
-            sides = [above[2:3, :], above[3:4, :], below[0:1, :], below[1:2, :]]
-            for q in range(4):
-                column = rows_in[d, 64 + 8 * q : 72 + 8 * q, :].astype(jnp.int32)
-                values[0, 8 * q : 8 * q + 8, :] = rows_in[d, 8 * q : 8 * q + 8, :] + rows_in[
-                    d, 32 + 8 * q : 40 + 8 * q, :
-                ] * edge_lookup(sides, column)
-            total[...] += scatter_sum(
-                lambda j: codes[pl.ds(8 * j + d, 1), :], lambda j: values[0, j : j + 1, :]
-            )
-
-        source = halves(total[...])
-        win_rhs[mine, :] = source + own[...]
+            pair = (lax.rem(rest, 8), lax.rem(rest // 8, 8))
+            for d in pair:
+                to_ocean(d).wait_recv()
+            for k, d in enumerate(pair):
+                above, here, below = edges.at[7 - d], edges.at[8 - d], edges.at[9 - d]
+                sides = [
+                    here[4:5, :] + above[2:3, :],
+                    here[5:6, :] + above[3:4, :],
+                    here[6:7, :] + below[0:1, :],
+                    here[7:8, :] + below[1:2, :],
+                ]
+                for q in range(4):
+                    column = rows_in[d, 32 + 8 * q : 40 + 8 * q, :].astype(jnp.int32)
+                    factor = jnp.where(column < INNER, edge_lookup(sides, column), 1.0)
+                    values[k, 8 * q : 8 * q + 8, :] = rows_in[d, 8 * q : 8 * q + 8, :] * factor
+            sums = [
+                scatter_sum(
+                    lambda j: codes[pl.ds(8 * j + d, 1), :], lambda j: values[k, j : j + 1, :], by_parity
+                )
+                for k, d in enumerate(pair)
+            ]
+            total[...] += sums[0] + sums[1]
+            return rest // 64
+
+        lax.fori_loop(0, SPAN // 2, take, row_order)
+        both = total[0:32] + total[32:64]
+        for k in (0, 1):
+            for h, x in enumerate(even_odd(own, 8 * k)):
+                part = slice(16 * h + 8 * k, 16 * h + 8 * k + 8)
+                win_rhs[h, OWN + 8 * k : OWN + 8 * k + 8, :] = both[part] + x
+                table[8 * k : 8 * k + 8, h * LANES : (h + 1) * LANES] = x - 0.25 * both[part]
         sides = to_windows(
-            lambda first, rows: win_rhs.at[pl.ds(OWN + first, rows)], win_rhs, rhs_send, rhs_recv
+            lambda first, rows: win_rhs.at[:, pl.ds(OWN + first, rows)],
+            lambda place, rows: win_rhs.at[:, pl.ds(place, rows)],
+            rhs_send,
+            rhs_recv,
         )
         for item in sides:
             item.start()
-        for item in ahead + sides:
+        for item in ahead:
             item.wait_recv()
-
-        def sweeps(eta, count, margin):
-            rows = WINDOW - 2 * margin
-            part = pl.ds(margin, rows)
-            skip = (eta.shape[0] - rows) // 2
-            code = win_code[part, :]
-            far = code >= 3
-            side = code - jnp.where(far, 3, 0)
-            from_up = pltpu.roll(side, rows - 1, 0)
-            from_down = pltpu.roll(side, 1, 0)
-            scale = 1.0 / (win_diag[part, :] + 3.0)
-            rhs = win_rhs[part, :]
-
-            def one(_, x):
-                left = pltpu.roll(x, 1, 1)
-                right = pltpu.roll(x, COLS - 1, 1)
-                up = jnp.where(from_up == 0, left, jnp.where(from_up == 1, x, right))
-                down = jnp.where(from_down == 0, left, jnp.where(from_down == 1, x, right))
-                third = jnp.where(far, pltpu.roll(down, rows - 1, 0), pltpu.roll(up, 1, 0))
-                return (rhs + (left + right + third)) * scale
-
-            return lax.fori_loop(0, count, one, eta[skip : skip + rows])
-
-        eta = win_rhs[...] / (win_diag[...] + 3.0)
-        eta = sweeps(eta, 3, 0)
-        eta = sweeps(eta, 8, 8)
-        eta = sweeps(eta, 8, 16)
-        eta = eta[8:24]
-        table[...] = own[...] + 0.5 * eta - 0.25 * source
-
-        @pl.loop(0, SPAN)
-        def _(i):
-            d = ahead_first(i)
+        for k in range(WINDOW // 8):
+            for h, x in enumerate(even_odd(win_diag, 8 * k)):
+                scale[h, 8 * k : 8 * k + 8, :] = 1.0 / (x + 3.0)
+            for h, x in enumerate(even_odd(win_code, 8 * k)):
+                turns[h, 8 * k : 8 * k + 8, :] = x
+        at_tile = [pl.ds(FIRST + i, 8, stride=DEPTH) for i in range(DEPTH)]
+        for h in (0, 1):
+            for i in range(DEPTH):
+                code = turns[h, at_tile[i], :]
+                ahead_row = jnp.where(code >= 3, 1, 0)
+                tile_far[h, i] = ahead_row
+                tile_side[h, i] = code - 3 * ahead_row
+                tile_scale[h, i] = scale[h, at_tile[i], :]
+        for item in sides:
+            item.wait_recv()
+        for h in (0, 1):
+            for i in range(DEPTH):
+                tile_first[h, i] = win_rhs[h, at_tile[i], :] * tile_scale[h, i]
+
+        def sweep(_, eta):
+            even, odd = list(eta[:DEPTH]), list(eta[DEPTH:])
+            before = [pltpu.roll(x, 1, 1) for x in odd]
+            after = [pltpu.roll(x, LANES - 1, 1) for x in even]
+
+            def extended(x):
+                return [pltpu.roll(x[-1], 1, 0)] + x + [pltpu.roll(x[0], 7, 0)]
+
+            even, odd, before, after = map(extended, (even, odd, before, after))
+            result = []
+            for h, (left, middle, right) in enumerate(((before, even, odd), (even, odd, after))):
+                for i in range(DEPTH):
+                    far = tile_far[h, i] == 1
+                    side = tile_side[h, i]
+                    x, y, z = (jnp.where(far, v[i + 2], v[i]) for v in (left, middle, right))
+                    third = jnp.where(side == 0, x, jnp.where(side == 1, y, z))
+                    near = left[i + 1] + right[i + 1] + third
+                    result.append(tile_first[h, i] + near * tile_scale[h, i])
+            return tuple(result)
+
+        eta = tuple(tile_first[h, i] for h in (0, 1) for i in range(DEPTH))
+        eta = lax.fori_loop(0, SWEEPS - 1, sweep, eta)
+        for h in (0, 1):
+            for i in range(DEPTH):
+                scale[h, at_tile[i], :] = eta[DEPTH * h + i]
+        mine_eta = [scale[h, OWN : OWN + ROWS, :] for h in (0, 1)]
+        table[...] = table[...] + 0.5 * jnp.concatenate(mine_eta, axis=1)
+        back = (3, 2, 0, 1, 6, 7, 5, 4)
+        rest = in_order((5, 6, 7, 2, 0, 1, 3, 4), back, back)
+        for _ in range(SPAN):
+            d = lax.rem(rest, 8)
+            rest = rest // 8
             for q in range(4):
-                rows_out[d, 8 * q : 8 * q + 8, :] = lookup(table, slab(codes, d, q))
+                rows_out[d, 8 * q : 8 * q + 8, :] = lookup(table, slab(codes, d, q), by_parity)
             to_air(d).start()
 
-        out[...] = eta
+        for k in (0, 1):
+            rows = slice(8 * k, 8 * k + 8)
+            out[rows, :] = interleaved(mine_eta[0][rows], mine_eta[1][rows])
         for item in ahead + sides:
             item.wait_send()
         for d in range(SPAN):
@@ -447,13 +527,19 @@
             pltpu.VMEM((SPAN + 2, 8, LANES), F32),
             pltpu.VMEM((len(MERGED), BLOCKS, LANES), jnp.int32),
             pltpu.VMEM((len(MERGED), BLOCKS, LANES), F32),
-            pltpu.VMEM((SPAN, 3 * BLOCKS, LANES), F32),
-            pltpu.VMEM((SPAN, 3 * BLOCKS, LANES), F32),
+            pltpu.VMEM((SPAN, 2 * BLOCKS, LANES), F32),
+            pltpu.VMEM((SPAN, 2 * BLOCKS, LANES), F32),
             pltpu.VMEM((64, LANES), F32),
             pltpu.VMEM((64, LANES), F32),
-            pltpu.VMEM((WINDOW, COLS), F32),
+            pltpu.VMEM((2, WINDOW, LANES), F32),
             pltpu.VMEM((WINDOW, COLS), F32),
             pltpu.VMEM((WINDOW, COLS), jnp.int32),
+            pltpu.VMEM((2, WINDOW, LANES), F32),
+            pltpu.VMEM((2, WINDOW, LANES), jnp.int32),
+            pltpu.VMEM((2, DEPTH, 8, LANES), F32),
+            pltpu.VMEM((2, DEPTH, 8, LANES), F32),
+            pltpu.VMEM((2, DEPTH, 8, LANES), jnp.int32),
+            pltpu.VMEM((2, DEPTH, 8, LANES), jnp.int32),
             dma((4,)),
             dma((SPAN + 2,)),
             dma((SPAN + 2,)),

time: 32.9 us -> 31.3 us (0.951)
  Pallas kernels: 32.2 us -> 30.5 us
    pallas_call x1, Pallas kernels: 32.2 us -> 30.5 us  [shards(): pl.pallas_call(kernel, out_shape=jax.ShapeDtypeStruct((ROWS, COLS), F32),...]
where the time goes in v4:
time: 31.3 us; the launch traced here: 31.1 us
  Pallas kernels  30.5 us (97%)
  local copies, waits for them, and re-layouts  0.61 us (2%)
    pallas_call x1, Pallas kernels, shards(): pl.pallas_call(kernel, out_shape=jax.ShapeDtypeStruct((ROWS, COLS), F32),...  30.5 us

profile of v4, /device:TPU:0, one launch (start us, length us, event | category | flops | bytes accessed | tf_op | source)
XLA Modules:
  0.0 31.1 jit_solution(16072723871786572106)
XLA Ops:
  0.0 30.5 %shard_map.64 = f32[16,256]{1,0:T(8,128)S(1)} custom-call(f32[1,16,256]{2,1,0:T(8,128)} %state.1, f32[1,16,256]{2,1,0:T(8,128)} %coeff.1, s32[16,256]{1,0:T(8,128)} %vertical.1, s32[256,128]{1,0:T(8,128)} %bitcast.17, s32[256,128]{1,0:T(8,128)} %bitcast.18, f32[256,128]{1,0:T(8,128)} %bitcast.19), custom_call_target="tpu_custom_call" | custom-call | tf_op jit(solution)/shard_map/pallas_call | solution.py:515
  30.5 0.6 %copy.8 = f32[1,16,256]{2,1,0:T(8,128)} copy(f32[1,16,256]{2,1,0:T(8,128)S(1)} %bitcast.16) | data formatting | bytes 32768

commit v5 on v4

--- a/solution.py
+++ b/solution.py
@@ -19,8 +19,7 @@
 OWN = 24
 INNER = 2 * COLS
 WINDOW = 64
-FIRST = 4
-DEPTH = 7
+STAGES = ((7, 8), (5, 8), (3, 3))
 MESH = pl.DeviceIdType.MESH
 F32 = jnp.float32
 BF16 = jnp.bfloat16
@@ -247,7 +246,7 @@
         ]
         for item in loads:
             item.start()
-        greet([(1, at(4 - e)) for e in range(SPAN + 2)])
+        greet([(1, at(offset)) for offset in (1, 2, 3, 4, -1, -2, -3, -4, -5, 0)])
         for item in loads[:2]:
             item.wait()
         s = own[...]
@@ -301,27 +300,32 @@
 
         share = 1.0 / halves(weight_sum[...])
         order = (2, 0, 1, 4, 3)
-        for m, n in zip(order, order[::-1]):
-
-            def either(x, y):
-                return x + is_first * (y - x)
-
-            d = either(MERGED[m][0], MERGED[n][0])
-            to_air(d).wait_recv()
-            pair = MERGED[m][1] is not None
-            if pair:
-                e = either(MERGED[m][1], MERGED[n][1])
-                to_air(e).wait_recv()
-            for q in range(4):
-                v = slab(weights, d, q) * rows_in[d, 8 * q : 8 * q + 8, :]
-                if pair:
-                    p = 3 - q
-                    v = v + reverse_tile(slab(weights, e, p) * rows_in[e, 8 * p : 8 * p + 8, :])
-                values[0, 8 * q : 8 * q + 8, :] = v
-            which = either(m, n)
-            total[...] += scatter_sum(
-                lambda j: merged[which, j : j + 1, :], lambda j: values[0, j : j + 1, :]
-            )
+        steps = list(enumerate(zip(order, order[::-1])))
+
+        def either(x, y):
+            return x + is_first * (y - x)
+
+        for group in (steps[:1], steps[1:2], steps[2:]):
+            ready = []
+            for k, (m, n) in group:
+                ends = [
+                    either(x, y) for x, y in zip(MERGED[m], MERGED[n]) if x is not None
+                ]
+                for d in ends:
+                    to_air(d).wait_recv()
+                ready.append((k, either(m, n), ends))
+            for k, _, ends in ready:
+                for q in range(4):
+                    d, p = ends[0], 3 - q
+                    v = slab(weights, d, q) * rows_in[d, 8 * q : 8 * q + 8, :]
+                    if len(ends) == 2:
+                        e = ends[1]
+                        v = v + reverse_tile(slab(weights, e, p) * rows_in[e, 8 * p : 8 * p + 8, :])
+                    values[k, 8 * q : 8 * q + 8, :] = v
+            for k, which, _ in ready:
+                total[...] += scatter_sum(
+                    lambda j: merged[which, j : j + 1, :], lambda j: values[k, j : j + 1, :]
+                )
         out[...] = halves(total[...]) * share
         for e in range(SPAN + 2):
             edge_to_ocean(e).wait_send()
@@ -340,8 +344,9 @@
         for item in loads:
             item.start()
         greet(
-            [(0, at(e - 4)) for e in range(SPAN + 2)]
-            + [(1, at(1)), (1, at(-1)), (1, at(2)), (1, at(-2))]
+            [(1, at(1)), (1, at(2))]
+            + [(0, at(offset)) for offset in (1, 2, 3, 4, 5, -1, -2, -3, -4, 0)]
+            + [(1, at(-1)), (1, at(-2))]
         )
 
         def to_windows(source, target, send, recv):
@@ -446,22 +451,27 @@
                 scale[h, 8 * k : 8 * k + 8, :] = 1.0 / (x + 3.0)
             for h, x in enumerate(even_odd(win_code, 8 * k)):
                 turns[h, 8 * k : 8 * k + 8, :] = x
-        at_tile = [pl.ds(FIRST + i, 8, stride=DEPTH) for i in range(DEPTH)]
-        for h in (0, 1):
-            for i in range(DEPTH):
-                code = turns[h, at_tile[i], :]
-                ahead_row = jnp.where(code >= 3, 1, 0)
-                tile_far[h, i] = ahead_row
-                tile_side[h, i] = code - 3 * ahead_row
-                tile_scale[h, i] = scale[h, at_tile[i], :]
+        def tiles(depth):
+            return [pl.ds(OWN + ROWS // 2 - 4 * depth + i, 8, stride=depth) for i in range(depth)]
+
+        for n, (depth, _) in enumerate(STAGES):
+            for h in (0, 1):
+                for i, rows in enumerate(tiles(depth)):
+                    code = turns[h, rows, :]
+                    ahead_row = jnp.where(code >= 3, 1, 0)
+                    tile_far[n, h, i] = ahead_row
+                    tile_side[n, h, i] = code - 3 * ahead_row
+                    tile_scale[n, h, i] = scale[h, rows, :]
         for item in sides:
             item.wait_recv()
-        for h in (0, 1):
-            for i in range(DEPTH):
-                tile_first[h, i] = win_rhs[h, at_tile[i], :] * tile_scale[h, i]
-
-        def sweep(_, eta):
-            even, odd = list(eta[:DEPTH]), list(eta[DEPTH:])
+        for n, (depth, _) in enumerate(STAGES):
+            for h in (0, 1):
+                for i, rows in enumerate(tiles(depth)):
+                    tile_first[n, h, i] = win_rhs[h, rows, :] * tile_scale[n, h, i]
+
+        def sweep(n, eta):
+            depth = STAGES[n][0]
+            even, odd = list(eta[:depth]), list(eta[depth:])
             before = [pltpu.roll(x, 1, 1) for x in odd]
             after = [pltpu.roll(x, LANES - 1, 1) for x in even]
 
@@ -471,27 +481,35 @@
             even, odd, before, after = map(extended, (even, odd, before, after))
             result = []
             for h, (left, middle, right) in enumerate(((before, even, odd), (even, odd, after))):
-                for i in range(DEPTH):
-                    far = tile_far[h, i] == 1
-                    side = tile_side[h, i]
+                for i in range(depth):
+                    far = tile_far[n, h, i] == 1
+                    side = tile_side[n, h, i]
                     x, y, z = (jnp.where(far, v[i + 2], v[i]) for v in (left, middle, right))
                     third = jnp.where(side == 0, x, jnp.where(side == 1, y, z))
                     near = left[i + 1] + right[i + 1] + third
-                    result.append(tile_first[h, i] + near * tile_scale[h, i])
+                    result.append(tile_first[n, h, i] + near * tile_scale[n, h, i])
             return tuple(result)
 
-        eta = tuple(tile_first[h, i] for h in (0, 1) for i in range(DEPTH))
-        eta = lax.fori_loop(0, SWEEPS - 1, sweep, eta)
-        for h in (0, 1):
-            for i in range(DEPTH):
-                scale[h, at_tile[i], :] = eta[DEPTH * h + i]
+        for n, (depth, count) in enumerate(STAGES):
+            if n == 0:
+                eta = tuple(tile_first[0, h, i] for h in (0, 1) for i in range(depth))
+            else:
+                eta = tuple(scale[h, rows, :] for h in (0, 1) for rows in tiles(depth))
+            for _ in range(count):
+                eta = sweep(n, eta)
+            for h in (0, 1):
+                for i, rows in enumerate(tiles(depth)):
+                    scale[h, rows, :] = eta[depth * h + i]
         mine_eta = [scale[h, OWN : OWN + ROWS, :] for h in (0, 1)]
         table[...] = table[...] + 0.5 * jnp.concatenate(mine_eta, axis=1)
-        back = (3, 2, 0, 1, 6, 7, 5, 4)
-        rest = in_order((5, 6, 7, 2, 0, 1, 3, 4), back, back)
-        for _ in range(SPAN):
+        start = is_last * (3 - lax.rem(tile, 4))
+        back = (3, 2, 1, 0, 6, 7, 5, 4)
+        rest = in_order((5, 6, 7, 2, 0, 1, 3, 4), (3, 2, 0, 1, 6, 7, 5, 4), back)
+        for k in range(SPAN):
             d = lax.rem(rest, 8)
             rest = rest // 8
+            if k < 4:
+                d = d + is_last * (lax.rem(d - start + 4, 4) - d)
             for q in range(4):
                 rows_out[d, 8 * q : 8 * q + 8, :] = lookup(table, slab(codes, d, q), by_parity)
             to_air(d).start()
@@ -536,10 +554,10 @@
             pltpu.VMEM((WINDOW, COLS), jnp.int32),
             pltpu.VMEM((2, WINDOW, LANES), F32),
             pltpu.VMEM((2, WINDOW, LANES), jnp.int32),
-            pltpu.VMEM((2, DEPTH, 8, LANES), F32),
-            pltpu.VMEM((2, DEPTH, 8, LANES), F32),
-            pltpu.VMEM((2, DEPTH, 8, LANES), jnp.int32),
-            pltpu.VMEM((2, DEPTH, 8, LANES), jnp.int32),
+            pltpu.VMEM((len(STAGES), 2, STAGES[0][0], 8, LANES), F32),
+            pltpu.VMEM((len(STAGES), 2, STAGES[0][0], 8, LANES), F32),
+            pltpu.VMEM((len(STAGES), 2, STAGES[0][0], 8, LANES), jnp.int32),
+            pltpu.VMEM((len(STAGES), 2, STAGES[0][0], 8, LANES), jnp.int32),
             dma((4,)),
             dma((SPAN + 2,)),
             dma((SPAN + 2,)),

time: 31.3 us -> 30.6 us (0.978)
  Pallas kernels: 30.5 us -> 29.8 us
    pallas_call x1, Pallas kernels: 30.5 us -> 29.8 us  [shards(): pl.pallas_call(kernel, out_shape=jax.ShapeDtypeStruct((ROWS, COLS), F32),...]
where the time goes in v5:
time: 30.6 us; the launch traced here: 30.5 us
  Pallas kernels  29.8 us (97%)
  local copies, waits for them, and re-layouts  0.61 us (2%)
    pallas_call x1, Pallas kernels, shards(): pl.pallas_call(kernel, out_shape=jax.ShapeDtypeStruct((ROWS, COLS), F32),...  29.8 us

profile of v5, /device:TPU:0, one launch (start us, length us, event | category | flops | bytes accessed | tf_op | source)
XLA Modules:
  0.0 30.5 jit_solution(18250741890977778000)
XLA Ops:
  0.0 29.8 %shard_map.64 = f32[16,256]{1,0:T(8,128)S(1)} custom-call(f32[1,16,256]{2,1,0:T(8,128)} %state.1, f32[1,16,256]{2,1,0:T(8,128)} %coeff.1, s32[16,256]{1,0:T(8,128)} %vertical.1, s32[256,128]{1,0:T(8,128)} %bitcast.17, s32[256,128]{1,0:T(8,128)} %bitcast.18, f32[256,128]{1,0:T(8,128)} %bitcast.19), custom_call_target="tpu_custom_call" | custom-call | tf_op jit(solution)/shard_map/pallas_call | solution.py:533
  29.8 0.6 %copy.8 = f32[1,16,256]{2,1,0:T(8,128)} copy(f32[1,16,256]{2,1,0:T(8,128)S(1)} %bitcast.16) | data formatting | bytes 32768

commit v6 on v5

--- a/solution.py
+++ b/solution.py
@@ -223,15 +223,8 @@
         return middle + is_first * (first - middle) + is_last * (last - middle)
 
     row_order = in_order(
-        (3, 2, 1, 0, 4, 5, 6, 7), (3, 5, 2, 6, 1, 7, 0, 4), (5, 6, 7, 4, 0, 3, 2, 1)
+        (3, 2, 1, 0, 4, 5, 6, 7), (5, 6, 7, 2, 4, 3, 0, 1), (5, 6, 7, 4, 0, 3, 2, 1)
     )
-
-    def for_each(order, body):
-        def step(i, rest):
-            body(i, lax.rem(rest, 8))
-            return rest // 8
-
-        lax.fori_loop(0, SPAN, step, order)
 
     def slab(ref, d, q):
         return ref[pl.ds(64 * q + d, 8, stride=8), :]
@@ -263,7 +256,10 @@
         ]
         for item in loads[2:]:
             item.wait()
-        for m, (d, e) in enumerate(MERGED):
+        def either(x, y):
+            return x + is_first * (y - x)
+
+        def prepare(m, d, e):
             for q in range(4):
                 part = slice(8 * q, 8 * q + 8)
                 cell = slab(codes, d, q)
@@ -285,10 +281,27 @@
                     rows_out[e, 32 + 8 * p : 40 + 8 * p, :] = reverse_tile(place)
                     w = w + reverse_tile(x)
                 values[m, part, :] = w
+
+        def prepare_all(pairs):
+            for x, y in pairs:
+                prepare(
+                    either(x, y),
+                    either(MERGED[x][0], MERGED[y][0]),
+                    None if MERGED[x][1] is None else either(MERGED[x][1], MERGED[y][1]),
+                )
+
+        order = list(zip((3, 4, 1, 2, 0), (2, 1, 0, 3, 4)))
+        sent = (5, 6, 7, 2, 4, 3, 0, 1)
+        rest = in_order((3, 2, 1, 0, 4, 5, 6, 7), sent, sent)
+        prepare_all(order[:3])
         met(SPAN + 2)
         for e in range(SPAN + 2):
             edge_to_ocean(e).start()
-        for_each(row_order, lambda i, d: to_ocean(d).start())
+        for k in range(SPAN):
+            if k == 5:
+                prepare_all(order[3:])
+            to_ocean(lax.rem(rest, 8)).start()
+            rest = rest // 8
         weight_sum[...] = jnp.zeros_like(weight_sum)
         total[...] = jnp.zeros_like(total)
 
@@ -301,9 +314,6 @@
         share = 1.0 / halves(weight_sum[...])
         order = (2, 0, 1, 4, 3)
         steps = list(enumerate(zip(order, order[::-1])))
-
-        def either(x, y):
-            return x + is_first * (y - x)
 
         for group in (steps[:1], steps[1:2], steps[2:]):
             ready = []
@@ -495,8 +505,7 @@
                 eta = tuple(tile_first[0, h, i] for h in (0, 1) for i in range(depth))
             else:
                 eta = tuple(scale[h, rows, :] for h in (0, 1) for rows in tiles(depth))
-            for _ in range(count):
-                eta = sweep(n, eta)
+            eta = lax.fori_loop(0, count, lambda _, x: sweep(n, x), eta)
             for h in (0, 1):
                 for i, rows in enumerate(tiles(depth)):
                     scale[h, rows, :] = eta[depth * h + i]
@@ -505,15 +514,18 @@
         start = is_last * (3 - lax.rem(tile, 4))
         back = (3, 2, 1, 0, 6, 7, 5, 4)
         rest = in_order((5, 6, 7, 2, 0, 1, 3, 4), (3, 2, 0, 1, 6, 7, 5, 4), back)
-        for k in range(SPAN):
-            d = lax.rem(rest, 8)
-            rest = rest // 8
-            if k < 4:
-                d = d + is_last * (lax.rem(d - start + 4, 4) - d)
-            for q in range(4):
-                rows_out[d, 8 * q : 8 * q + 8, :] = lookup(table, slab(codes, d, q), by_parity)
-            to_air(d).start()
-
+        def give(i, rest):
+            for k in range(2):
+                d = lax.rem(rest, 8)
+                rest = rest // 8
+                back_turn = is_last * ((SPAN - 1 - (2 * i + k)) // 4)
+                d = d + back_turn * (lax.rem(d - start + 4, 4) - d)
+                for q in range(4):
+                    rows_out[d, 8 * q : 8 * q + 8, :] = lookup(table, slab(codes, d, q), by_parity)
+                to_air(d).start()
+            return rest
+
+        lax.fori_loop(0, SPAN // 2, give, rest)
         for k in (0, 1):
             rows = slice(8 * k, 8 * k + 8)
             out[rows, :] = interleaved(mine_eta[0][rows], mine_eta[1][rows])

time: 30.6 us -> 30.4 us (level)
  no operation moved by 1% of the time
where the time goes in v6:
time: 30.4 us; the launch traced here: 30.3 us
  Pallas kernels  29.7 us (98%)
  local copies, waits for them, and re-layouts  0.61 us (2%)
    pallas_call x1, Pallas kernels, shards(): pl.pallas_call(kernel, out_shape=jax.ShapeDtypeStruct((ROWS, COLS), F32),...  29.7 us

profile of v6, /device:TPU:0, one launch (start us, length us, event | category | flops | bytes accessed | tf_op | source)
XLA Modules:
  0.0 30.3 jit_solution(17330044310299267068)
XLA Ops:
  0.0 29.7 %shard_map.64 = f32[16,256]{1,0:T(8,128)S(1)} custom-call(f32[1,16,256]{2,1,0:T(8,128)} %state.1, f32[1,16,256]{2,1,0:T(8,128)} %coeff.1, s32[16,256]{1,0:T(8,128)} %vertical.1, s32[256,128]{1,0:T(8,128)} %bitcast.17, s32[256,128]{1,0:T(8,128)} %bitcast.18, f32[256,128]{1,0:T(8,128)} %bitcast.19), custom_call_target="tpu_custom_call" | custom-call | tf_op jit(solution)/shard_map/pallas_call | solution.py:545
  29.7 0.6 %copy.8 = f32[1,16,256]{2,1,0:T(8,128)} copy(f32[1,16,256]{2,1,0:T(8,128)S(1)} %bitcast.16) | data formatting | bytes 32768

commit v7 on v6

--- a/solution.py
+++ b/solution.py
@@ -315,7 +315,7 @@
         order = (2, 0, 1, 4, 3)
         steps = list(enumerate(zip(order, order[::-1])))
 
-        for group in (steps[:1], steps[1:2], steps[2:]):
+        for group in (steps[:2], steps[2:]):
             ready = []
             for k, (m, n) in group:
                 ends = [
@@ -332,10 +332,11 @@
                         e = ends[1]
                         v = v + reverse_tile(slab(weights, e, p) * rows_in[e, 8 * p : 8 * p + 8, :])
                     values[k, 8 * q : 8 * q + 8, :] = v
-            for k, which, _ in ready:
-                total[...] += scatter_sum(
-                    lambda j: merged[which, j : j + 1, :], lambda j: values[k, j : j + 1, :]
-                )
+            sums = [
+                scatter_sum(lambda j: merged[which, j : j + 1, :], lambda j: values[k, j : j + 1, :])
+                for k, which, _ in ready
+            ]
+            total[...] += sum(sums[1:], sums[0])
         out[...] = halves(total[...]) * share
         for e in range(SPAN + 2):
             edge_to_ocean(e).wait_send()

time: 30.4 us -> 30.4 us (level)
  no operation moved by 1% of the time
where the time goes in v7:
time: 30.4 us; the launch traced here: 30.3 us
  Pallas kernels  29.7 us (98%)
  local copies, waits for them, and re-layouts  0.61 us (2%)
    pallas_call x1, Pallas kernels, shards(): pl.pallas_call(kernel, out_shape=jax.ShapeDtypeStruct((ROWS, COLS), F32),...  29.7 us

profile of v7, /device:TPU:0, one launch (start us, length us, event | category | flops | bytes accessed | tf_op | source)
XLA Modules:
  0.0 30.3 jit_solution(7571864509015437632)
XLA Ops:
  0.0 29.7 %shard_map.64 = f32[16,256]{1,0:T(8,128)S(1)} custom-call(f32[1,16,256]{2,1,0:T(8,128)} %state.1, f32[1,16,256]{2,1,0:T(8,128)} %coeff.1, s32[16,256]{1,0:T(8,128)} %vertical.1, s32[256,128]{1,0:T(8,128)} %bitcast.17, s32[256,128]{1,0:T(8,128)} %bitcast.18, f32[256,128]{1,0:T(8,128)} %bitcast.19), custom_call_target="tpu_custom_call" | custom-call | tf_op jit(solution)/shard_map/pallas_call | solution.py:546
  29.7 0.6 %copy.8 = f32[1,16,256]{2,1,0:T(8,128)} copy(f32[1,16,256]{2,1,0:T(8,128)S(1)} %bitcast.16) | data formatting | bytes 32768

commit v8 on v7

--- a/solution.py
+++ b/solution.py
@@ -352,13 +352,13 @@
             load(coeff.at[0], win_diag.at[mine], 2),
             load(vertical, win_code.at[mine], 3),
         ]
-        for item in loads:
-            item.start()
         greet(
             [(1, at(1)), (1, at(2))]
             + [(0, at(offset)) for offset in (1, 2, 3, 4, 5, -1, -2, -3, -4, 0)]
             + [(1, at(-1)), (1, at(-2))]
         )
+        for item in loads:
+            item.start()
 
         def to_windows(source, target, send, recv):
             return [

time: 30.4 us -> 30.4 us (level)
  no operation moved by 1% of the time
where the time goes in v8:
time: 30.4 us; the launch traced here: 30.2 us
  Pallas kernels  29.6 us (97%)
  local copies, waits for them, and re-layouts  0.61 us (2%)
    pallas_call x1, Pallas kernels, shards(): pl.pallas_call(kernel, out_shape=jax.ShapeDtypeStruct((ROWS, COLS), F32),...  29.6 us

profile of v8, /device:TPU:0, one launch (start us, length us, event | category | flops | bytes accessed | tf_op | source)
XLA Modules:
  0.0 30.2 jit_solution(13883885367516955693)
XLA Ops:
  0.0 29.6 %shard_map.64 = f32[16,256]{1,0:T(8,128)S(1)} custom-call(f32[1,16,256]{2,1,0:T(8,128)} %state.1, f32[1,16,256]{2,1,0:T(8,128)} %coeff.1, s32[16,256]{1,0:T(8,128)} %vertical.1, s32[256,128]{1,0:T(8,128)} %bitcast.17, s32[256,128]{1,0:T(8,128)} %bitcast.18, f32[256,128]{1,0:T(8,128)} %bitcast.19), custom_call_target="tpu_custom_call" | custom-call | tf_op jit(solution)/shard_map/pallas_call | solution.py:546
  29.6 0.6 %copy.8 = f32[1,16,256]{2,1,0:T(8,128)} copy(f32[1,16,256]{2,1,0:T(8,128)S(1)} %bitcast.16) | data formatting | bytes 32768
